TPU v7x, 32 devices: a whole 2x2x4 slice. The times are simulated.
32 devices in a mesh: bins: 16 (over z, y, x), params: 2 (over core).
Axes of the slice: x: 2, y: 2, z: 4, core: 2. Of those that a mesh axis runs over, the one named last changes fastest.
Arguments:
- event_bins: int32 [49152], P('bins'), may hold values from 0 to 16383, as said below
- event_weights: bfloat16 [49152, 3072], P('bins', 'params'), may hold values from -6 to 6
- nominal: bfloat16 [49152], P('bins'), may hold values from 0.5 to 2
- background: float32 [16384], P('bins'), may hold values from 1 to 10
- observed: float32 [16384], P('bins'), may hold values from 1 to 100
Outputs:
- hessian: float32 [3072, 3072], P(('params', 'bins'))
Inputs may be any that keep to these rules, and one draw needn't show every extreme that they name: `event_bins`: each index of bins holds 3072 consecutive events in ascending bin order. The owner of bin b is b // 1024; each owner's bins receive from one index of bins between 96 and 288 of its events, and in every draw every index of bins has some owner that receives exactly 288 of its events.
All inputs are finite; a program needn't handle non-finite values.
Results may differ from a plain program's by a relative error of at most 0.0016.
Values may be sent and summed in bfloat16 or wider, within the bound.
A program may use at most 128 MiB of HBM per device.

v0:
```python
import functools
import math

import jax
import jax.numpy as jnp
from jax import lax
from jax.experimental import pallas as pl
from jax.experimental.pallas import tpu as pltpu
from jax.sharding import PartitionSpec as P

ALIGN = 8
MESH = pl.DeviceIdType.MESH


def from_behind(value, axis, steps):
    count = lax.axis_size(axis)
    pairs = [(source, (source + steps) % count) for source in range(count)]
    return lax.ppermute(value, axis, pairs)


def pack_kernel(owners, slot, first, width, starts_ref, rows_ref, out_ref, held, in_sems, out_sems):
    def fetch(o):
        start = pl.multiple_of(starts_ref[o] * ALIGN, ALIGN)
        return pltpu.make_async_copy(
            rows_ref.at[pl.ds(start, slot), pl.ds(first, width)], held.at[o], in_sems.at[o]
        )

    def store(o):
        return pltpu.make_async_copy(held.at[o], out_ref.at[o], out_sems.at[o])

    @pl.loop(0, owners)
    def _(o):
        fetch(o).start()

    @pl.loop(0, owners)
    def _(o):
        fetch(o).wait()
        store(o).start()

    @pl.loop(0, owners)
    def _(o):
        store(o).wait()


def pack(starts, rows, slot, first, width):
    owners = starts.shape[0]
    return pl.pallas_call(
        functools.partial(pack_kernel, owners, slot, first, width),
        out_shape=jax.ShapeDtypeStruct((owners, slot, width), rows.dtype),
        in_specs=[
            pl.BlockSpec(memory_space=pltpu.SMEM),
            pl.BlockSpec(memory_space=pl.ANY),
        ],
        out_specs=pl.BlockSpec(memory_space=pl.ANY),
        scratch_shapes=[
            pltpu.VMEM((owners, slot, width), rows.dtype),
            pltpu.SemaphoreType.DMA((owners,)),
            pltpu.SemaphoreType.DMA((owners,)),
        ],
        compiler_params=pltpu.CompilerParams(vmem_limit_bytes=32 << 20),
        cost_estimate=pl.CostEstimate(
            flops=0, bytes_accessed=4 * owners * slot * width, transcendentals=0
        ),
        name="pack",
    )(starts, rows)


def meta_kernel(bins_dev, starts_ref, table_ref, out_ref):
    owners, _, slot = out_ref.shape
    events = table_ref.shape[1]
    table = table_ref[...]

    @pl.loop(0, owners)
    def _(o):
        start = starts_ref[o] * ALIGN
        turned = pltpu.roll(table, lax.rem(events - start, events), axis=1)[:, :slot]
        bins = turned[0:1] - (o * bins_dev).astype(jnp.float32)
        inside = (bins >= 0) & (bins < bins_dev)
        out_ref[o, 0:1, :] = jnp.where(inside, bins, -1.0)
        out_ref[o, 1:2, :] = turned[1:2]


def pack_meta(starts, table, slot, bins_dev):
    owners = starts.shape[0]
    return pl.pallas_call(
        functools.partial(meta_kernel, bins_dev),
        out_shape=jax.ShapeDtypeStruct((owners, 2, slot), jnp.float32),
        in_specs=[
            pl.BlockSpec(memory_space=pltpu.SMEM),
            pl.BlockSpec(memory_space=pltpu.VMEM),
        ],
        out_specs=pl.BlockSpec(memory_space=pltpu.VMEM),
        name="pack_meta",
    )(starts, table)


def hist_kernel(chunk, tile, local_ref, rows_ref, out_ref, hot):
    bins, total = hot.shape

    @pl.when(pl.program_id(0) == 0)
    def _():
        ids = lax.broadcasted_iota(jnp.int32, (bins, chunk), 0)

        @pl.loop(0, total // chunk)
        def _(k):
            part = pl.ds(pl.multiple_of(k * chunk, chunk), chunk)
            hot[:, part] = (ids == local_ref[:, part]).astype(jnp.bfloat16)

    @pl.loop(0, bins // tile)
    def _(m):
        part = pl.ds(pl.multiple_of(m * tile, tile), tile)
        out_ref[part, :] = jnp.dot(
            hot[part, :], rows_ref[...], preferred_element_type=jnp.float32
        ).astype(out_ref.dtype)


def histogram_of(local, rows, bins, block, dtype):
    total, width = rows.shape
    return pl.pallas_call(
        functools.partial(hist_kernel, math.gcd(total, 128), math.gcd(bins, 256)),
        grid=(width // block,),
        out_shape=jax.ShapeDtypeStruct((bins, width), dtype),
        in_specs=[
            pl.BlockSpec((1, total), lambda j: (0, 0)),
            pl.BlockSpec((total, block), lambda j: (0, j)),
        ],
        out_specs=pl.BlockSpec((bins, block), lambda j: (0, j)),
        scratch_shapes=[pltpu.VMEM((bins, total), jnp.bfloat16)],
        compiler_params=pltpu.CompilerParams(
            vmem_limit_bytes=40 << 20, dimension_semantics=("arbitrary",)
        ),
        cost_estimate=pl.CostEstimate(
            flops=2 * bins * total * width, bytes_accessed=2 * total * width, transcendentals=0
        ),
        name="histogram",
    )(local, rows)


def reduce_kernel(
    piece, shares_ref, out_ref, own, got_near, sums, got_far,
    own_sem, near_send, near_recv, far_send, far_recv,
):
    far, near, rows, _ = shares_ref.shape
    me = lax.axis_index("bins")
    f, n = me // near, lax.rem(me, near)

    def near_peer(d):
        return lax.rem(n + d, near)

    def far_peer(d):
        return lax.rem(f + d, far)

    barrier = pltpu.get_barrier_semaphore()
    for d in range(1, near):
        pl.semaphore_signal(
            barrier, inc=1, device_id={"bins": f * near + near_peer(d)}, device_id_type=MESH
        )
    for d in range(1, far):
        pl.semaphore_signal(
            barrier, inc=1, device_id={"bins": far_peer(d) * near + n}, device_id_type=MESH
        )
    pl.semaphore_wait(barrier, near + far - 2)

    def part_of(c):
        return pl.ds(pl.multiple_of(c * piece, piece), piece)

    def near_copy(d, c):
        return pltpu.make_async_remote_copy(
            src_ref=shares_ref.at[:, near_peer(d), part_of(c), :],
            dst_ref=got_near.at[d - 1, :, part_of(c), :],
            send_sem=near_send.at[d - 1, c],
            recv_sem=near_recv.at[d - 1, c],
            device_id={"bins": f * near + near_peer(d)},
            device_id_type=MESH,
        )

    def far_copy(d, c):
        return pltpu.make_async_remote_copy(
            src_ref=sums.at[far_peer(d), part_of(c), :],
            dst_ref=got_far.at[d - 1, part_of(c), :],
            send_sem=far_send.at[d - 1, c],
            recv_sem=far_recv.at[d - 1, c],
            device_id={"bins": far_peer(d) * near + n},
            device_id_type=MESH,
        )

    own_copy = pltpu.make_async_copy(shares_ref.at[:, n], own, own_sem)
    own_copy.start()
    pieces = rows // piece

    @pl.loop(0, pieces)
    def _(c):
        for d in range(1, near):
            near_copy(d, c).start()

    own_copy.wait()

    @pl.loop(0, pieces)
    def _(c):
        part = part_of(c)
        for d in range(1, near):
            near_copy(d, c).wait_recv()

        @pl.loop(0, far)
        def _(k):
            total = own[k, part, :].astype(jnp.float32)
            for d in range(1, near):
                total += got_near[d - 1, k, part, :].astype(jnp.float32)
            sums[k, part, :] = total

        for d in range(1, far):
            far_copy(d, c).start()

    @pl.loop(0, pieces)
    def _(c):
        part = part_of(c)
        for d in range(1, far):
            far_copy(d, c).wait_recv()
        total = sums[f, part, :]
        for d in range(1, far):
            total += got_far[d - 1, part, :]
        out_ref[part, :] = total
        for d in range(1, near):
            near_copy(d, c).wait_send()
        for d in range(1, far):
            far_copy(d, c).wait_send()


def reduce_shares(shares):
    owners, rows, cols = shares.shape
    near = math.isqrt(owners)
    while owners % near:
        near -= 1
    far = owners // near
    piece = 16 if rows % 16 == 0 else rows
    pieces = rows // piece
    return pl.pallas_call(
        functools.partial(reduce_kernel, piece),
        out_shape=jax.ShapeDtypeStruct((rows, cols), jnp.float32),
        in_specs=[pl.BlockSpec(memory_space=pl.ANY)],
        out_specs=pl.BlockSpec(memory_space=pltpu.VMEM),
        scratch_shapes=[
            pltpu.VMEM((far, rows, cols), shares.dtype),
            pltpu.VMEM((near - 1, far, rows, cols), shares.dtype),
            pltpu.VMEM((far, rows, cols), jnp.float32),
            pltpu.VMEM((far - 1, rows, cols), jnp.float32),
            pltpu.SemaphoreType.DMA,
            pltpu.SemaphoreType.DMA((near - 1, pieces)),
            pltpu.SemaphoreType.DMA((near - 1, pieces)),
            pltpu.SemaphoreType.DMA((far - 1, pieces)),
            pltpu.SemaphoreType.DMA((far - 1, pieces)),
        ],
        compiler_params=pltpu.CompilerParams(
            collective_id=1, has_side_effects=True, vmem_limit_bytes=40 << 20
        ),
        name="reduce_shares",
    )(shares.reshape(far, near, rows, cols))


def body(event_bins, event_weights, nominal, background, observed):
    owners = lax.axis_size("bins")
    groups_count = lax.axis_size("params")
    events = event_bins.shape[0]
    width_g = event_weights.shape[1]
    bins_dev = background.shape[0]
    capacity = 3 * events // (2 * owners)
    slot = -(-capacity // ALIGN) * ALIGN + ALIGN
    chunks = 2 if width_g % 512 == 0 else 1
    width = width_g // chunks
    block = math.gcd(width, 256)

    destination = event_bins // bins_dev
    targets = jnp.arange(owners, dtype=jnp.int32)
    before = jnp.sum((destination[None, :] < targets[:, None]).astype(jnp.int32), axis=1)
    starts = jnp.minimum(before // ALIGN, (events - slot) // ALIGN)

    table = jnp.stack([event_bins.astype(jnp.float32), nominal.astype(jnp.float32)])
    table = jnp.concatenate([table, jnp.zeros((6, events), jnp.float32)], axis=0)
    meta = pack_meta(starts, table, slot, bins_dev)
    got_meta = lax.all_to_all(meta, "bins", split_axis=0, concat_axis=0, tiled=True)
    local = got_meta[:, 0].astype(jnp.int32).reshape(1, owners * slot)
    got_nominal = got_meta[:, 1].astype(jnp.bfloat16).reshape(owners * slot, 1)
    got_nominal = jnp.broadcast_to(got_nominal, (owners * slot, 128))
    nominal_sum = histogram_of(local, got_nominal, bins_dev, 128, jnp.float32)[:, 0]
    yields = background + nominal_sum
    curvature = observed / (yields * yields)

    parts = []
    for c in range(chunks):
        packed = pack(starts, event_weights, slot, c * width, width)
        got = lax.all_to_all(packed, "bins", split_axis=0, concat_axis=0, tiled=True)
        got = got.reshape(owners * slot, width)
        parts.append(histogram_of(local, got, bins_dev, block, jnp.bfloat16))
    templates = jnp.concatenate(parts, axis=1)
    weighted = (curvature[:, None] * templates.astype(jnp.float32)).astype(jnp.bfloat16)
    pieces = [templates]
    for shift_by in range(1, groups_count // 2 + 1):
        shifted = [from_behind(part, "params", -shift_by) for part in parts]
        pieces.append(jnp.concatenate(shifted, axis=1))
    partners = jnp.concatenate(pieces, axis=1)
    dims = (((0,), (0,)), ((), ()))
    full = lax.dot_general(weighted, partners, dims, preferred_element_type=jnp.float32)
    full = full.astype(jnp.bfloat16)
    shares = full.reshape(owners, width_g // owners, full.shape[1])
    summed = reduce_shares(shares)
    return summed * (1.0 / (bins_dev * owners))


def solution(mesh):
    in_specs = (P("bins"), P("bins", "params"), P("bins"), P("bins"), P("bins"))
    out_specs = P(("params", "bins"), None)
    return jax.shard_map(body, mesh=mesh, in_specs=in_specs, out_specs=out_specs, check_vma=False)
```

profile of v0, /device:TPU:28, one launch (start us, length us, event | category | flops | bytes accessed | tf_op | source)
XLA Modules:
  0.0 528.6 jit_solution(3968735147014836358)
XLA Ops:
  0.0 0.7 stack.12
  0.7 0.8 fusion.17
  2.3 0.7 maximum_maximum_fusion.table_ref
  3.0 3.4 pack_meta.1
  6.3 6.9 %all-to-all-start = ((f32[16,2,296]{2,1,0:T(2,128)}), f32[16,2,296]{2,1,0:T(2,128)S(1)}, u32[]{:S(2)}, u32[]{:S(2)}) async-start(f32[16,2,296]{2,1,0:T(2,128)} %pack_meta.1), calls=%async_computation | async-start | bytes 98304 | tf_op jit(solution)/shard_map/all_to_all | solution.py:280
  13.3 3.7 copy-done
  17.0 0.6 copy-done.5
  17.6 6.0 %pack.3 = bf16[16,296,768]{2,1,0:T(8,128)(2,1)S(1)} custom-call(s32[16]{0:T(128)S(1)} %copy-done.5, bf16[3072,1536]{1,0:T(8,128)(2,1)S(1)} %copy-done), custom_call_target="tpu_custom_call" | custom-call | bytes 14548992 | tf_op jit(solution)/shard_map/pack/pallas_call | solution.py:47
  23.6 3.0 copy-done.3
  26.6 6.9 %all-to-all-start.2 = ((bf16[16,296,768]{2,1,0:T(8,128)(2,1)}), bf16[16,296,768]{2,1,0:T(8,128)(2,1)}, u32[]{:S(2)}, u32[]{:S(2)}) async-start(bf16[16,296,768]{2,1,0:T(8,128)(2,1)} %copy-done.3), calls=%async_computation.2 | async-start | bytes 14548992 | tf_op jit(solution)/shard_map/all_to_all | solution.py:291
  33.5 3.7 copy-done.1
  37.2 6.0 %pack.2 = bf16[16,296,768]{2,1,0:T(8,128)(2,1)S(1)} custom-call(s32[16]{0:T(128)S(1)} %copy-done.6, bf16[3072,1536]{1,0:T(8,128)(2,1)S(1)} %copy-done.1), custom_call_target="tpu_custom_call" | custom-call | bytes 14548992 | tf_op jit(solution)/shard_map/pack/pallas_call | solution.py:47
  43.2 2.9 copy-done.2
  46.1 150.7 %all-to-all-done.2 = bf16[16,296,768]{2,1,0:T(8,128)(2,1)} async-done(((bf16[16,296,768]{2,1,0:T(8,128)(2,1)}), bf16[16,296,768]{2,1,0:T(8,128)(2,1)}, u32[]{:S(2)}, u32[]{:S(2)}) %all-to-all-start.2) | async-done | bytes 7274528 | tf_op jit(solution)/shard_map/all_to_all | solution.py:291
  196.8 6.0 %all-to-all-start.1 = ((bf16[16,296,768]{2,1,0:T(8,128)(2,1)}), bf16[16,296,768]{2,1,0:T(8,128)(2,1)}, u32[]{:S(2)}, u32[]{:S(2)}) async-start(bf16[16,296,768]{2,1,0:T(8,128)(2,1)} %copy-done.2), calls=%async_computation.1 | async-start | bytes 14548992 | tf_op jit(solution)/shard_map/all_to_all | solution.py:291
  203.1 14.1 %histogram.5 = bf16[1024,768]{1,0:T(8,128)(2,1)S(1)} custom-call(s32[1,4736]{1,0:T(1,128)S(1)} %convert_element_type.40.local_ref, bf16[4736,768]{1,0:T(8,128)(2,1)} %bitcast.3.rows_ref), custom_call_target="tpu_custom_call" | custom-call | flops 7449083904 | bytes 7274496 | tf_op jit(solution)/shard_map/histogram/pallas_call | solution.py:119
  217.3 144.3 %all-to-all-done.1 = bf16[16,296,768]{2,1,0:T(8,128)(2,1)} async-done(((bf16[16,296,768]{2,1,0:T(8,128)(2,1)}), bf16[16,296,768]{2,1,0:T(8,128)(2,1)}, u32[]{:S(2)}, u32[]{:S(2)}) %all-to-all-start.1) | async-done | bytes 7274528 | tf_op jit(solution)/shard_map/all_to_all | solution.py:291
  361.6 14.2 %histogram.4 = bf16[1024,768]{1,0:T(8,128)(2,1)S(1)} custom-call(s32[1,4736]{1,0:T(1,128)S(1)} %convert_element_type.40.local_ref, bf16[4736,768]{1,0:T(8,128)(2,1)} %bitcast.2.rows_ref), custom_call_target="tpu_custom_call" | custom-call | flops 7449083904 | bytes 7274496 | tf_op jit(solution)/shard_map/histogram/pallas_call | solution.py:119
  376.1 2.3 broadcast_in_dim.5.rows_ref
  378.4 5.6 %histogram.3 = f32[1024,128]{1,0:T(8,128)S(1)} custom-call(s32[1,4736]{1,0:T(1,128)S(1)} %convert_element_type.40.local_ref, bf16[4736,128]{1,0:T(8,128)(2,1)S(1)} %broadcast_in_dim.5.rows_ref), custom_call_target="tpu_custom_call" | custom-call | flops 1241513984 | bytes 1212416 | tf_op jit(solution)/shard_map/histogram/pallas_call | solution.py:119
  384.3 13.8 %convolution_convert_fusion = bf16[1536,3072]{1,0:T(8,128)(2,1)} fusion(bf16[1024,768]{1,0:T(8,128)(2,1)} %collective-permute-done.1, bf16[1024,768]{1,0:T(8,128)(2,1)} %collective-permute-done, bf16[1024,768]{1,0:T(8,128)(2,1)S(1)} %histogram.5, bf16[1024,768]{1,0:T(8,128)(2,1)S(1)} %histogram.4, f32[1024]{0:T(1024)S(1)} %multiply_divide_fusion), kind=kOutput, calls=%fused_computation | convolution fusion | flops 9702998016 | bytes 15732736 | tf_op jit(solution)/shard_map/dot_general | solution.py:302
  398.2 3.7 copy-done.4
  401.9 125.6 %reduce_shares.1 = f32[96,3072]{1,0:T(8,128)S(1)} custom-call(bf16[4,4,96,3072]{3,2,1,0:T(8,128)(2,1)S(1)} %bitcast.5), custom_call_target="tpu_custom_call" | custom-call | tf_op jit(solution)/shard_map/reduce_shares/pallas_call | solution.py:237
  527.5 1.1 broadcast_multiply_fusion
  (27 shorter events, 1.5 us)
Async XLA Ops:
  6.3 20.3 %all-to-all-start = ((f32[16,2,296]{2,1,0:T(2,128)}), f32[16,2,296]{2,1,0:T(2,128)S(1)}, u32[]{:S(2)}, u32[]{:S(2)}) async-start(f32[16,2,296]{2,1,0:T(2,128)} %pack_meta.1), calls=%async_computation | async-start | bytes 98304 | tf_op jit(solution)/shard_map/all_to_all | solution.py:280
  13.3 3.7 copy-start
  17.0 0.6 copy-start.5
  23.6 3.0 copy-start.3
  26.6 6.9 %copy-start.6 = (s32[16]{0:T(128)S(1)}, s32[16]{0:T(128)}, u32[]{:S(2)}) copy-start(s32[16]{0:T(128)} %fusion.15.starts_ref) | copy-start | bytes 196
  26.6 170.3 %all-to-all-start.2 = ((bf16[16,296,768]{2,1,0:T(8,128)(2,1)}), bf16[16,296,768]{2,1,0:T(8,128)(2,1)}, u32[]{:S(2)}, u32[]{:S(2)}) async-start(bf16[16,296,768]{2,1,0:T(8,128)(2,1)} %copy-done.3), calls=%async_computation.2 | async-start | bytes 14548992 | tf_op jit(solution)/shard_map/all_to_all | solution.py:291
  33.5 3.7 copy-start.1
  43.2 2.9 copy-start.2
  196.8 164.7 %all-to-all-start.1 = ((bf16[16,296,768]{2,1,0:T(8,128)(2,1)}), bf16[16,296,768]{2,1,0:T(8,128)(2,1)}, u32[]{:S(2)}, u32[]{:S(2)}) async-start(bf16[16,296,768]{2,1,0:T(8,128)(2,1)} %copy-done.2), calls=%async_computation.1 | async-start | bytes 14548992 | tf_op jit(solution)/shard_map/all_to_all | solution.py:291
  217.2 167.1 %collective-permute-start.1 = (bf16[1024,768]{1,0:T(8,128)(2,1)S(1)}, bf16[1024,768]{1,0:T(8,128)(2,1)}, u32[]{:S(2)}, u32[]{:S(2)}) collective-permute-start(bf16[1024,768]{1,0:T(8,128)(2,1)S(1)} %histogram.5), channel_id=1, source_target_pairs={{0,1},{1,0},{2,3},{3,2},{4,5},{5,4},{6,7},{7,6},{8,9},{9,8},{10,11... | collective-permute-start | bytes 4718600 | tf_op jit(solution)/shard_map/ppermute | solution.py:18
  375.8 8.5 %copy-start.7 = (f32[1024]{0:T(1024)S(1)}, f32[1024]{0:T(1024)}, u32[]{:S(2)}) copy-start(f32[1024]{0:T(1024)} %param.9) | copy-start | bytes 12292
  375.8 8.5 %copy-start.8 = (f32[1024]{0:T(1024)S(1)}, f32[1024]{0:T(1024)}, u32[]{:S(2)}) copy-start(f32[1024]{0:T(1024)} %param.8) | copy-start | bytes 12292
  375.8 8.5 %collective-permute-start = (bf16[1024,768]{1,0:T(8,128)(2,1)S(1)}, bf16[1024,768]{1,0:T(8,128)(2,1)}, u32[]{:S(2)}, u32[]{:S(2)}) collective-permute-start(bf16[1024,768]{1,0:T(8,128)(2,1)S(1)} %histogram.4), channel_id=1, source_target_pairs={{0,1},{1,0},{2,3},{3,2},{4,5},{5,4},{6,7},{7,6},{8,9},{9,8},{10,11... | collective-permute-start | bytes 4718600 | tf_op jit(solution)/shard_map/ppermute | solution.py:18
  398.2 3.7 copy-start.4
where the time goes:
time: 529 us
  waiting for transfers between devices  295 us (56%)
  Pallas kernels  175 us (33%)
  local copies, waits for them, and re-layouts  20.5 us (4%)
  starting transfers between devices  20 us (4%)
  matrix products  13.8 us (3%)
    all_to_all x2, waiting for transfers between devices, body(): lax.all_to_all(packed, 'bins', split_axis=0, concat_axis=0, tiled=True)  295 us
    pallas_call x1, Pallas kernels, reduce_shares(): pl.pallas_call(functools.partial(reduce_kernel, piece), out_shape=jax.Sha...  126 us
    pallas_call x3, Pallas kernels, histogram_of(): pl.pallas_call(functools.partial(hist_kernel, math.gcd(total, 128), math....  34 us
    unnamed x18, local copies, waits for them, and re-layouts  17.6 us
    dot_general x1, matrix products, body(): lax.dot_general(weighted, partners, dims, preferred_element_type=jnp.floa...  13.8 us
    all_to_all x2, starting transfers between devices, body(): lax.all_to_all(packed, 'bins', split_axis=0, concat_axis=0, tiled=True)  12.9 us
    pallas_call x2, Pallas kernels, pack(): pl.pallas_call(functools.partial(pack_kernel, owners, slot, first, width)...  12 us
  transfers between devices with their start and end apart: 5, of which 2 were waited for; matrix products, arithmetic and copies ran while one was open for 1% of the time, Pallas kernels for 9%

commit v1 on v0

--- a/solution.py
+++ b/solution.py
@@ -306,7 +306,457 @@
     return summed * (1.0 / (bins_dev * owners))
 
 
+LANES = 128
+TILE = 256
+
+
+def shift(value, pairs):
+    return lax.ppermute(value, "bins", pairs)
+
+
+def xor_of(a, b, count):
+    total, bit = 0, 1
+    while bit < count:
+        total = total + bit * lax.rem(a // bit + b // bit, 2)
+        bit *= 2
+    return total
+
+
+def diagonal():
+    rows = lax.broadcasted_iota(jnp.int32, (LANES, LANES), 0)
+    return rows == lax.broadcasted_iota(jnp.int32, (LANES, LANES), 1)
+
+
+def fold_kernel(sources, steps, received, last, info_ref, before_ref, ids_ref, *refs):
+    rows_refs = refs[:sources]
+    got = refs[sources : sources + 2 * received]
+    outs = refs[sources + 2 * received : -1]
+    acc = refs[-1]
+    events = ids_ref.shape[1]
+    block = outs[0].shape[0]
+    tiles = block // TILE
+    bounds = before_ref.shape[0] // sources
+
+    @pl.when(info_ref[1] == 1)
+    def _():
+        @pl.loop(0, tiles)
+        def _(k):
+            index = (info_ref[0] * steps + pl.program_id(0)) * tiles + k
+            bins = index * TILE + lax.broadcasted_iota(jnp.int32, (TILE, LANES), 0)
+
+            def product(s, start):
+                ids = ids_ref[s : s + 1, pl.ds(start, LANES)]
+                hot = (bins == ids).astype(jnp.bfloat16)
+                return jnp.dot(
+                    hot, rows_refs[s][pl.ds(start, LANES), :], preferred_element_type=jnp.float32
+                )
+
+            total = jnp.zeros((TILE, LANES), jnp.float32)
+            firsts = []
+            for s in range(sources):
+                low = before_ref[s * bounds + index]
+                first = jnp.minimum(low // LANES * LANES, events - 2 * LANES)
+                first = pl.multiple_of(first, LANES)
+                firsts.append(first)
+                total += product(s, first)
+                total += product(s, pl.multiple_of(first + LANES, LANES))
+            acc[...] = total
+            for s in range(sources):
+                high = before_ref[s * bounds + index + 1]
+                rest = jnp.maximum(high - firsts[s] - 2 * LANES + LANES - 1, 0) // LANES
+                begin = firsts[s] + 2 * LANES
+
+                @pl.loop(0, rest)
+                def _(e):
+                    acc[...] += product(s, pl.multiple_of(begin + e * LANES, LANES))
+
+            eye = diagonal()
+            for h in range(TILE // LANES):
+                line = k * (TILE // LANES) + h
+                part = pl.ds(pl.multiple_of(line * LANES, LANES), LANES)
+                value = acc[h * LANES : (h + 1) * LANES, :]
+                for n in range(received):
+                    scale = got[2 * n + 1][pl.ds(line, 1), :]
+                    scale = jnp.sum(jnp.where(eye, scale, 0.0), axis=1, keepdims=True)
+                    value += got[2 * n][part, :].astype(jnp.int32).astype(jnp.float32) * scale
+                if last:
+                    outs[0][part, :] = value.astype(outs[0].dtype)
+                else:
+                    most = jnp.max(jnp.abs(value), axis=1, keepdims=True)
+                    wide = most * (2.0**23 + 1.0)
+                    step = (wide + (most - wide)) * 2.0**-14
+                    factor = jnp.where(most > 1e-30, 1.0 / step, 0.0)
+                    coded = jnp.round(value * factor).astype(jnp.int32)
+                    outs[0][part, :] = coded.astype(outs[0].dtype)
+                    scale = jnp.where(eye, step, 0.0)
+                    outs[1][pl.ds(line, 1), :] = jnp.sum(scale, axis=0, keepdims=True)
+
+
+def fold(info, before, ids, rows, got, bins, last):
+    sources, events = ids.shape
+    block = 8 * LANES
+    steps = bins // block
+    smem = pl.BlockSpec(memory_space=pltpu.SMEM)
+    values = pl.BlockSpec((block, LANES), lambda j: (j, 0))
+    scales = pl.BlockSpec((8, LANES), lambda j: (j, 0))
+    whole_rows = pl.BlockSpec((events, LANES), lambda j: (0, 0))
+    flat = [part for pair in got for part in pair]
+    if last:
+        out_shape = [jax.ShapeDtypeStruct((bins, LANES), jnp.bfloat16)]
+        out_specs = [values]
+    else:
+        out_shape = [
+            jax.ShapeDtypeStruct((bins, LANES), jnp.int16),
+            jax.ShapeDtypeStruct((bins // LANES, LANES), jnp.float32),
+        ]
+        out_specs = [values, scales]
+    return pl.pallas_call(
+        functools.partial(fold_kernel, sources, steps, len(got), last),
+        grid=(steps,),
+        out_shape=out_shape,
+        in_specs=[smem, smem, pl.BlockSpec((sources, events), lambda j: (0, 0))]
+        + [whole_rows] * sources
+        + [values, scales] * len(got),
+        out_specs=out_specs,
+        scratch_shapes=[pltpu.VMEM((TILE, LANES), jnp.float32)],
+        compiler_params=pltpu.CompilerParams(
+            vmem_limit_bytes=24 << 20, dimension_semantics=("arbitrary",)
+        ),
+        cost_estimate=pl.CostEstimate(
+            flops=bins * 2 * sources * 256 * LANES,
+            bytes_accessed=2 * sources * events * LANES + 4 * bins * LANES,
+            transcendentals=0,
+        ),
+        name="fold_last" if last else "fold",
+    )(info, before, ids, *rows, *flat)
+
+
+def curve_kernel(lows_ref, ids_ref, nominal_ref, background_ref, observed_ref, out_ref, acc):
+    sources = ids_ref.shape[0]
+    bounds = lows_ref.shape[0] // sources
+    index = pl.program_id(0)
+    first_bin = lows_ref[sources * (bounds - 1)]
+    bins = first_bin + index * TILE + lax.broadcasted_iota(jnp.int32, (TILE, LANES), 0)
+    acc[...] = jnp.zeros_like(acc)
+
+    @pl.loop(0, sources)
+    def _(s):
+        low = lows_ref[s * (bounds - 1) + index]
+        high = lows_ref[s * (bounds - 1) + index + 1]
+
+        @pl.loop(low // LANES, (high + LANES - 1) // LANES)
+        def _(b):
+            part = pl.ds(pl.multiple_of(b * LANES, LANES), LANES)
+            hit = bins == ids_ref[s, :, part]
+            acc[...] += jnp.where(hit, nominal_ref[s, :, part], 0.0)
+
+    yields = background_ref[...] + jnp.sum(acc[...], axis=1, keepdims=True)
+    out_ref[...] = observed_ref[...] / (yields * yields)
+
+
+def curvature_of(lows, first_bin, ids, nominal, background, observed):
+    sources, events = ids.shape
+    bins = background.shape[0]
+    table = jnp.concatenate(
+        [lows.reshape(-1), first_bin.reshape(1), jnp.zeros((sources - 1,), jnp.int32)]
+    )
+    column = pl.BlockSpec((TILE, 1), lambda j: (j, 0))
+    whole = pl.BlockSpec((sources, 1, events), lambda j: (0, 0, 0))
+    return pl.pallas_call(
+        curve_kernel,
+        grid=(bins // TILE,),
+        out_shape=jax.ShapeDtypeStruct((bins, 1), jnp.float32),
+        in_specs=[pl.BlockSpec(memory_space=pltpu.SMEM), whole, whole, column, column],
+        out_specs=column,
+        scratch_shapes=[pltpu.VMEM((TILE, LANES), jnp.float32)],
+        compiler_params=pltpu.CompilerParams(
+            vmem_limit_bytes=8 << 20, dimension_semantics=("arbitrary",)
+        ),
+        name="curvature",
+    )(
+        table,
+        ids.reshape(sources, 1, events),
+        nominal.reshape(sources, 1, events),
+        background.reshape(bins, 1),
+        observed.reshape(bins, 1),
+    )
+
+
+def weigh_kernel(near, chunks, piece, me_ref, curve_ref, *refs):
+    out_ref = refs[-1]
+    rows = lax.broadcasted_iota(jnp.int32, (piece, LANES), 0) + me_ref[0] * piece
+    lanes = lax.broadcasted_iota(jnp.int32, (piece, LANES), 1)
+    for d in range(near):
+        total = 0.0
+        for c in range(chunks):
+            pick = (rows == lanes + c * LANES).astype(jnp.bfloat16)
+            value = curve_ref[...] * refs[d * chunks + c][...].astype(jnp.float32)
+            total += lax.dot_general(
+                pick, value.astype(jnp.bfloat16), (((1,), (1,)), ((), ())),
+                preferred_element_type=jnp.float32,
+            )
+        out_ref[d * piece : (d + 1) * piece, :] = total.astype(out_ref.dtype)
+
+
+def weigh(me, curve, templates, near, chunks, piece):
+    bins = curve.shape[0]
+    tile = 512
+    return pl.pallas_call(
+        functools.partial(weigh_kernel, near, chunks, piece),
+        grid=(bins // tile,),
+        out_shape=jax.ShapeDtypeStruct((near * piece, bins), jnp.bfloat16),
+        in_specs=[
+            pl.BlockSpec(memory_space=pltpu.SMEM),
+            pl.BlockSpec((tile, 1), lambda j: (j, 0)),
+        ]
+        + [pl.BlockSpec((tile, LANES), lambda j: (j, 0))] * (near * chunks),
+        out_specs=pl.BlockSpec((near * piece, tile), lambda j: (0, j)),
+        compiler_params=pltpu.CompilerParams(
+            vmem_limit_bytes=24 << 20, dimension_semantics=("arbitrary",)
+        ),
+        name="weigh",
+    )(me, curve, *templates)
+
+
+def hessian_kernel(count, weighted_ref, *refs):
+    pieces = refs[:count]
+    full_ref, coded_ref, held, sems = refs[count:]
+    bins = held.shape[0]
+    depth = math.gcd(bins, 1024)
+
+    def fetch(n):
+        return pltpu.make_async_copy(
+            pieces[n], held.at[:, n * LANES : (n + 1) * LANES], sems.at[n]
+        )
+
+    for n in range(count):
+        fetch(n).start()
+    for n in range(0, count, 2):
+        fetch(n).wait()
+        fetch(n + 1).wait()
+        columns = slice(n * LANES, (n + 2) * LANES)
+        total = jnp.dot(
+            weighted_ref[...], held[:, columns], preferred_element_type=jnp.float32
+        )
+        full_ref[:, columns] = total
+        coded_ref[:, columns] = total.astype(coded_ref.dtype)
+
+
+def hessian_of(weighted, pieces):
+    rows, bins = weighted.shape
+    count = len(pieces)
+    shape = (rows, count * LANES)
+    return pl.pallas_call(
+        functools.partial(hessian_kernel, count),
+        out_shape=[
+            jax.ShapeDtypeStruct(shape, jnp.float32),
+            jax.ShapeDtypeStruct(shape, jnp.bfloat16),
+        ],
+        in_specs=[pl.BlockSpec(memory_space=pltpu.VMEM)]
+        + [pl.BlockSpec(memory_space=pl.ANY)] * count,
+        out_specs=[pl.BlockSpec(memory_space=pltpu.VMEM)] * 2,
+        scratch_shapes=[
+            pltpu.VMEM((bins, count * LANES), jnp.bfloat16),
+            pltpu.SemaphoreType.DMA((count,)),
+        ],
+        compiler_params=pltpu.CompilerParams(vmem_limit_bytes=48 << 20),
+        cost_estimate=pl.CostEstimate(
+            flops=2 * rows * bins * count * LANES,
+            bytes_accessed=2 * bins * count * LANES,
+            transcendentals=0,
+        ),
+        name="hessian",
+    )(weighted, *pieces)
+
+
+def sum_kernel(near, far, piece, run, full_ref, coded_ref, out_ref, own, got, own_sem, sends, recvs):
+    here = lax.axis_index("bins")
+    z, me = here // near, lax.rem(here, near)
+    columns = out_ref.shape[1]
+
+    def peer(k):
+        return lax.rem(z + k, far)
+
+    barrier = pltpu.get_barrier_semaphore()
+    for k in range(1, far):
+        pl.semaphore_signal(
+            barrier, inc=1, device_id={"bins": peer(k) * near + me}, device_id_type=MESH
+        )
+    pl.semaphore_wait(barrier, far - 1)
+
+    def rows_for(target):
+        return pl.ds(pl.multiple_of(xor_of(me, target, near) * piece, piece), piece)
+
+    def copy(k):
+        return pltpu.make_async_remote_copy(
+            src_ref=coded_ref.at[rows_for(peer(k)), :],
+            dst_ref=got.at[k - 1],
+            send_sem=sends.at[k - 1],
+            recv_sem=recvs.at[k - 1],
+            device_id={"bins": peer(k) * near + me},
+            device_id_type=MESH,
+        )
+
+    for k in range(1, far):
+        copy(k).start()
+    own_copy = pltpu.make_async_copy(full_ref.at[rows_for(z), :], own, own_sem)
+    own_copy.start()
+    own_copy.wait()
+    for k in range(1, far):
+        copy(k).wait_recv()
+    for n in range(columns // run):
+        group, d = n // near, n % near
+        total = own[:, n * run : (n + 1) * run]
+        for k in range(1, far):
+            total += got[k - 1, :, n * run : (n + 1) * run].astype(jnp.float32)
+        start = (group * near + xor_of(me, d, near)) * run
+        out_ref[:, pl.ds(pl.multiple_of(start, LANES), run)] = total
+    for k in range(1, far):
+        copy(k).wait_send()
+
+
+def sum_over_planes(full, coded, near, far, run):
+    rows, columns = full.shape
+    piece = rows // far
+    return pl.pallas_call(
+        functools.partial(sum_kernel, near, far, piece, run),
+        out_shape=jax.ShapeDtypeStruct((piece, columns), jnp.float32),
+        in_specs=[pl.BlockSpec(memory_space=pl.ANY)] * 2,
+        out_specs=pl.BlockSpec(memory_space=pltpu.VMEM),
+        scratch_shapes=[
+            pltpu.VMEM((piece, columns), jnp.float32),
+            pltpu.VMEM((far - 1, piece, columns), coded.dtype),
+            pltpu.SemaphoreType.DMA,
+            pltpu.SemaphoreType.DMA((far - 1,)),
+            pltpu.SemaphoreType.DMA((far - 1,)),
+        ],
+        compiler_params=pltpu.CompilerParams(
+            collective_id=2, has_side_effects=True, vmem_limit_bytes=16 << 20
+        ),
+        name="sum_over_planes",
+    )(full, coded)
+
+
+def body_by_parameters(event_bins, event_weights, nominal, background, observed):
+    owners = lax.axis_size("bins")
+    near = math.isqrt(owners)
+    far = owners // near
+    events = event_bins.shape[0]
+    bins_dev = background.shape[0]
+    width = event_weights.shape[1] // near
+    chunks = width // LANES
+    bins = near * bins_dev
+    here = lax.axis_index("bins")
+    z, me = here // near, lax.rem(here, near)
+    planes = range(far)
+    around = [[(s, s // near * near + (s % near ^ d)) for s in range(owners)] for d in range(near)]
+
+    def spread(value):
+        return [value] + [shift(value, around[d]) for d in range(1, near)]
+
+    meta = jnp.concatenate([event_bins.astype(jnp.float32), nominal.astype(jnp.float32)])
+    meta = jnp.stack(spread(meta.reshape(2, events)))
+    local = jnp.stack(spread(jnp.stack([background, observed])))
+    ids = meta[:, 0].astype(jnp.int32)
+    marks = jnp.arange(far * bins // TILE + 1, dtype=jnp.int32) * TILE
+    before = jnp.sum((ids[:, None, :] < marks[None, :, None]).astype(jnp.int32), axis=2)
+    before = before.reshape(-1)
+
+    def chunk_of(weights, c):
+        parts = []
+        for d in range(near):
+            start = (me ^ d) * width + c * LANES
+            part = lax.dynamic_slice(weights, (0, start), (events, LANES))
+            parts.append(part if d == 0 else shift(part, around[d]))
+        return parts
+
+    def info(target):
+        valid = (target >= 0) & (target < far)
+        return jnp.stack([jnp.clip(target, 0, far - 1), valid.astype(jnp.int32)])
+
+    def up(r):
+        return [(p * near + m, (p + 1) * near + m) for p in planes if p < r for m in range(near)]
+
+    def down(r):
+        return [
+            (p * near + m, (p - 1) * near + m) for p in planes if p >= far - r for m in range(near)
+        ]
+
+    def send(pair, pairs):
+        return tuple(shift(part, pairs) for part in pair)
+
+    rows_of = []
+    weights = event_weights
+    for c in range(chunks):
+        rows_of.append(chunk_of(weights, c))
+        weights, _ = lax.optimization_barrier((weights, rows_of[c][1:]))
+
+    own = [None] * chunks
+    for c in range(chunks):
+        rows = rows_of[c]
+        rising, falling = [], []
+        for r in range(1, far):
+            rising = [send(fold(info(z + far - r), before, ids, rows, rising, bins, False), up(r))]
+            falling = [
+                send(fold(info(z - far + r), before, ids, rows, falling, bins, False), down(r))
+            ]
+        own[c] = fold(info(z), before, ids, rows, rising + falling, bins, True)[0]
+
+    metas = [meta] + [
+        shift(meta, [(s, (s + k * near) % owners) for s in range(owners)]) for k in range(1, far)
+    ]
+    metas = jnp.concatenate(metas)
+    all_ids = metas[:, 0].astype(jnp.int32)
+    first_bin = z * bins
+    near_marks = first_bin + jnp.arange(bins // TILE + 1, dtype=jnp.int32) * TILE
+    lows = jnp.sum((all_ids[:, None, :] < near_marks[None, :, None]).astype(jnp.int32), axis=2)
+    places = jnp.arange(near, dtype=jnp.int32)
+    match = (places[None, :] ^ me) == places[:, None]
+    local = jnp.sum(jnp.where(match[:, :, None, None], local[None], 0.0), axis=1)
+    curve = curvature_of(
+        lows, first_bin, all_ids, metas[:, 1], local[:, 0].reshape(-1), local[:, 1].reshape(-1)
+    )
+
+    mine = [spread(own[c]) for c in range(chunks)]
+    mine = [mine[c][d] for d in range(near) for c in range(chunks)]
+    theirs = [from_behind(part, "params", 1) for part in mine]
+    weighted = weigh(
+        me.reshape(1).astype(jnp.int32), curve, mine, near, chunks, width // far
+    )
+    full, coded = hessian_of(weighted, mine + theirs)
+    summed = sum_over_planes(full, coded, near, far, width)
+    return summed * (1.0 / (bins_dev * owners))
+
+
+def splits_by_parameters(mesh, event_bins, event_weights, background):
+    owners, groups = mesh.shape["bins"], mesh.shape["params"]
+    near = math.isqrt(owners)
+    events = event_bins.shape[0] // owners
+    width = event_weights.shape[1] // groups // max(near, 1)
+    bins_dev = background.shape[0] // owners
+    return (
+        groups == 2
+        and near > 1
+        and near * near == owners
+        and near & (near - 1) == 0
+        and width % LANES == 0
+        and width % (16 * near) == 0
+        and events % LANES == 0
+        and events >= 2 * LANES
+        and bins_dev % (8 * LANES) == 0
+    )
+
+
 def solution(mesh):
     in_specs = (P("bins"), P("bins", "params"), P("bins"), P("bins"), P("bins"))
     out_specs = P(("params", "bins"), None)
-    return jax.shard_map(body, mesh=mesh, in_specs=in_specs, out_specs=out_specs, check_vma=False)
+
+    def run(event_bins, event_weights, nominal, background, observed):
+        fits = splits_by_parameters(mesh, event_bins, event_weights, background)
+        chosen = body_by_parameters if fits else body
+        mapped = jax.shard_map(
+            chosen, mesh=mesh, in_specs=in_specs, out_specs=out_specs, check_vma=False
+        )
+        return mapped(event_bins, event_weights, nominal, background, observed)
+
+    return run

time: 529 us -> 636 us (1.20)
  starting transfers between devices: 20 us -> 143 us
  waiting for transfers between devices: 295 us -> 193 us
  Pallas kernels: 175 us -> 261 us
  matrix products: 13.8 us -> 0 us
  local copies, waits for them, and re-layouts: 20.5 us -> 31.4 us
    all_to_all x3 -> x0, waiting for transfers between devices: 295 us -> none  [the longest x2 295 us: body(): lax.all_to_all(packed, 'bins', split_axis=0, concat_axis=0, tiled=True)]
    ppermute x0 -> x63, waiting for transfers between devices: none -> 193 us  [shift(): return lax.ppermute(value, 'bins', pairs)]
    ppermute x0 -> x63, starting transfers between devices: none -> 141 us  [shift(): return lax.ppermute(value, 'bins', pairs)]
    pallas_call x7 -> x25, Pallas kernels: 175 us -> 261 us  [the longest x21 155 us: fold(): pl.pallas_call(functools.partial(fold_kernel, sources, steps, len(got), l...]
    all_to_all x3 -> x0, starting transfers between devices: 19.9 us -> none  [the longest x2 12.9 us: body(): lax.all_to_all(packed, 'bins', split_axis=0, concat_axis=0, tiled=True)]
    dot_general x1 -> x0, matrix products: 13.8 us -> none  [body(): lax.dot_general(weighted, partners, dims, preferred_element_type=jnp.floa...]
    dynamic_slice x0 -> x3, local copies, waits for them, and re-layouts: none -> 10 us  [chunk_of(): part = lax.dynamic_slice(weights, (0, start), (events, LANES))]
    unnamed x18 -> x86, local copies, waits for them, and re-layouts: 17.6 us -> 14.8 us
  transfers between devices with their start and end apart: 5 -> 75, of which waited for: 2 -> 17; matrix products, arithmetic and copies ran while one was open for 1% -> 2% of each run, Pallas kernels for 9% -> 28%
where the time goes in v1:
time: 636 us; the launch traced here: 634 us
  Pallas kernels  261 us (41%)
  waiting for transfers between devices  193 us (30%)
  starting transfers between devices  143 us (22%)
  local copies, waits for them, and re-layouts  31.4 us (5%)
    ppermute x63, waiting for transfers between devices, shift(): return lax.ppermute(value, 'bins', pairs)  193 us
    pallas_call x21, Pallas kernels, fold(): pl.pallas_call(functools.partial(fold_kernel, sources, steps, len(got), l...  155 us
    ppermute x63, starting transfers between devices, shift(): return lax.ppermute(value, 'bins', pairs)  141 us
    pallas_call x1, Pallas kernels, sum_over_planes(): pl.pallas_call(functools.partial(sum_kernel, near, far, piece, run), out_...  55.6 us
    pallas_call x1, Pallas kernels, hessian_of(): pl.pallas_call(functools.partial(hessian_kernel, count), out_shape=[jax.S...  27.5 us
    unnamed x86, local copies, waits for them, and re-layouts  14.8 us
    pallas_call x1, Pallas kernels, curvature_of(): pl.pallas_call(curve_kernel, grid=(bins // TILE,), out_shape=jax.ShapeDty...  14.7 us
  transfers between devices with their start and end apart: 75, of which 17 were waited for; matrix products, arithmetic and copies ran while one was open for 2% of the time, Pallas kernels for 28%

profile of v1, /device:TPU:28, one launch (start us, length us, event | category | flops | bytes accessed | tf_op | source)
XLA Modules:
  0.0 633.9 jit_solution(14435459817994903472)
XLA Ops:
  10.1 31.6 %collective-permute-done.1 = f32[2,3072]{1,0:T(2,128)S(1)} collective-permute-done((f32[2,3072]{1,0:T(2,128)S(1)}, f32[2,3072]{1,0:T(2,128)S(1)}, u32[]{:S(2)}, u32[]{:S(2)}) %collective-permute-start.1) | collective-permute-done | bytes 24608 | tf_op jit(solution)/shard_map/ppermute | solution.py:314
  70.3 16.3 %collective-permute-done.7 = f32[2,1024]{1,0:T(2,128)S(1)} collective-permute-done((f32[2,1024]{1,0:T(2,128)S(1)}, f32[2,1024]{1,0:T(2,128)S(1)}, u32[]{:S(2)}, u32[]{:S(2)}) %collective-permute-start.7) | collective-permute-done | bytes 8224 | tf_op jit(solution)/shard_map/ppermute | solution.py:314
  90.7 10.3 %fold.27 = (s16[4096,128]{1,0:T(8,128)(2,1)}, f32[32,128]{1,0:T(8,128)S(1)}) custom-call(s32[2]{0:T(128)S(1)} %get-tuple-element.105.info_ref, s32[260]{0:T(512)S(1)} %reshape.55.before_ref, s32[4,3072]{1,0:T(4,128)S(1)} %fusion.ids_ref, bf16[3072,128]{1,0:T(8,128)(2,1)S(1)} %get-tuple-element.92.refs_0_, bf16[3072,128]{1,0:T(8,128)(2,1)} %collective-permute-done.24.refs_1_, ...), custom_call_target="tpu_custom_call" | custom-call | flops 1073741824 | bytes 5242880 | tf_op jit(solution)/shard_map/fold/pallas_call | solution.py:413
  101.1 15.5 %collective-permute-done.5 = f32[4,2,3072]{2,0,1:T(4,128)S(1)} collective-permute-done((f32[4,2,3072]{2,0,1:T(4,128)S(1)}, f32[4,2,3072]{2,0,1:T(4,128)S(1)}, u32[]{:S(2)}, u32[]{:S(2)}) %collective-permute-start.5) | collective-permute-done | bytes 98336 | tf_op jit(solution)/shard_map/ppermute | solution.py:314
  137.0 10.9 %fold.22 = (s16[4096,128]{1,0:T(8,128)(2,1)}, f32[32,128]{1,0:T(8,128)S(1)}) custom-call(s32[2]{0:T(128)S(1)} %pad_add_fusion.6.info_ref, s32[260]{0:T(512)S(1)} %reshape.55.before_ref, s32[4,3072]{1,0:T(4,128)S(1)} %fusion.ids_ref, bf16[3072,128]{1,0:T(8,128)(2,1)S(1)} %get-tuple-element.96.refs_0_, bf16[3072,128]{1,0:T(8,128)(2,1)S(1)} %copy-done.7, ...), custom_call_target="tpu_custom_call" | custom-call | flops 1073741824 | bytes 5242880 | tf_op jit(solution)/shard_map/fold/pallas_call | solution.py:413
  152.6 10.4 %collective-permute-done.40.refs_2_ = bf16[3072,128]{1,0:T(8,128)(2,1)} collective-permute-done((bf16[3072,128]{1,0:T(8,128)(2,1)}, bf16[3072,128]{1,0:T(8,128)(2,1)}, u32[]{:S(2)}, u32[]{:S(2)}) %collective-permute-start.40) | collective-permute-done | bytes 786464 | tf_op jit(solution)/shard_map/ppermute | solution.py:314
  166.0 10.4 %fold.33 = (s16[4096,128]{1,0:T(8,128)(2,1)}, f32[32,128]{1,0:T(8,128)S(1)}) custom-call(s32[2]{0:T(128)S(1)} %get-tuple-element.105.info_ref, s32[260]{0:T(512)S(1)} %reshape.55.before_ref, s32[4,3072]{1,0:T(4,128)S(1)} %fusion.ids_ref, bf16[3072,128]{1,0:T(8,128)(2,1)S(1)} %get-tuple-element.88.refs_0_, bf16[3072,128]{1,0:T(8,128)(2,1)} %collective-permute-done.39.refs_1_, ...), custom_call_target="tpu_custom_call" | custom-call | flops 1073741824 | bytes 5242880 | tf_op jit(solution)/shard_map/fold/pallas_call | solution.py:413
  195.4 11.6 %fold.28 = (s16[4096,128]{1,0:T(8,128)(2,1)}, f32[32,128]{1,0:T(8,128)S(1)}) custom-call(s32[2]{0:T(128)S(1)} %pad_add_fusion.6.info_ref, s32[260]{0:T(512)S(1)} %reshape.55.before_ref, s32[4,3072]{1,0:T(4,128)S(1)} %fusion.ids_ref, bf16[3072,128]{1,0:T(8,128)(2,1)S(1)} %get-tuple-element.92.refs_0_, bf16[3072,128]{1,0:T(8,128)(2,1)} %collective-permute-done.24.refs_1_, ...), custom_call_target="tpu_custom_call" | custom-call | flops 1073741824 | bytes 5242880 | tf_op jit(solution)/shard_map/fold/pallas_call | solution.py:413
  225.9 10.9 %fold.23 = (s16[4096,128]{1,0:T(8,128)(2,1)}, f32[32,128]{1,0:T(8,128)S(1)}) custom-call(s32[2]{0:T(128)S(1)} %pad_add_fusion.5.info_ref, s32[260]{0:T(512)S(1)} %reshape.55.before_ref, s32[4,3072]{1,0:T(4,128)S(1)} %fusion.ids_ref, bf16[3072,128]{1,0:T(8,128)(2,1)S(1)} %get-tuple-element.96.refs_0_, bf16[3072,128]{1,0:T(8,128)(2,1)S(1)} %copy-done.8, ...), custom_call_target="tpu_custom_call" | custom-call | flops 1073741824 | bytes 5242880 | tf_op jit(solution)/shard_map/fold/pallas_call | solution.py:413
  243.3 15.7 %collective-permute-start.22 = (s16[4096,128]{1,0:T(8,128)(2,1)}, s16[4096,128]{1,0:T(8,128)(2,1)}, u32[]{:S(2)}, u32[]{:S(2)}) collective-permute-start(s16[4096,128]{1,0:T(8,128)(2,1)} %get-tuple-element.55), channel_id=1, source_target_pairs={{8,0},{10,2},{12,4},{14,6},{16,8},{18,10},{20,12},{22,14},{24,16},... | collective-permute-start | bytes 3145736 | tf_op jit(solution)/shard_map/ppermute | solution.py:314
  260.3 11.7 %fold.34 = (s16[4096,128]{1,0:T(8,128)(2,1)}, f32[32,128]{1,0:T(8,128)S(1)}) custom-call(s32[2]{0:T(128)S(1)} %pad_add_fusion.6.info_ref, s32[260]{0:T(512)S(1)} %reshape.55.before_ref, s32[4,3072]{1,0:T(4,128)S(1)} %fusion.ids_ref, bf16[3072,128]{1,0:T(8,128)(2,1)S(1)} %get-tuple-element.88.refs_0_, bf16[3072,128]{1,0:T(8,128)(2,1)} %collective-permute-done.39.refs_1_, ...), custom_call_target="tpu_custom_call" | custom-call | flops 1073741824 | bytes 5242880 | tf_op jit(solution)/shard_map/fold/pallas_call | solution.py:413
  283.2 18.9 %collective-permute-start.50 = (s16[4096,128]{1,0:T(8,128)(2,1)}, s16[4096,128]{1,0:T(8,128)(2,1)}, u32[]{:S(2)}, u32[]{:S(2)}) collective-permute-start(s16[4096,128]{1,0:T(8,128)(2,1)} %get-tuple-element.79), channel_id=1, source_target_pairs={{16,8},{18,10},{20,12},{22,14},{24,16},{26,18},{28,20},{30,22},{17... | collective-permute-start | bytes 3145736 | tf_op jit(solution)/shard_map/ppermute | solution.py:314
  303.8 10.9 %fold.29 = (s16[4096,128]{1,0:T(8,128)(2,1)S(1)}, f32[32,128]{1,0:T(8,128)S(1)}) custom-call(s32[2]{0:T(128)S(1)} %pad_add_fusion.5.info_ref, s32[260]{0:T(512)S(1)} %reshape.55.before_ref, s32[4,3072]{1,0:T(4,128)S(1)} %fusion.ids_ref, bf16[3072,128]{1,0:T(8,128)(2,1)S(1)} %get-tuple-element.92.refs_0_, bf16[3072,128]{1,0:T(8,128)(2,1)} %collective-permute-done.24.refs_1_, ...), custom_call_target="tpu_custom_call" | custom-call | flops 1073741824 | bytes 5242880 | tf_op jit(solution)/shard_map/fold/pallas_call | solution.py:413
  320.6 10.5 %collective-permute-start.37 = (s16[4096,128]{1,0:T(8,128)(2,1)S(1)}, s16[4096,128]{1,0:T(8,128)(2,1)S(1)}, u32[]{:S(2)}, u32[]{:S(2)}) collective-permute-start(s16[4096,128]{1,0:T(8,128)(2,1)S(1)} %get-tuple-element.68), channel_id=1, source_target_pairs={{8,0},{10,2},{12,4},{14,6},{16,8},{18,10},{20,12},{22,14},{24,16},... | collective-permute-start | bytes 3145736 | tf_op jit(solution)/shard_map/ppermute | solution.py:314
  343.0 10.9 %collective-permute-done.32.refs_5_ = f32[32,128]{1,0:T(8,128)S(1)} collective-permute-done((f32[32,128]{1,0:T(8,128)S(1)}, f32[32,128]{1,0:T(8,128)S(1)}, u32[]{:S(2)}, u32[]{:S(2)}) %collective-permute-start.32) | collective-permute-done | bytes 16416 | tf_op jit(solution)/shard_map/ppermute | solution.py:314
  355.7 10.9 %fold.35 = (s16[4096,128]{1,0:T(8,128)(2,1)S(1)}, f32[32,128]{1,0:T(8,128)S(1)}) custom-call(s32[2]{0:T(128)S(1)} %pad_add_fusion.5.info_ref, s32[260]{0:T(512)S(1)} %reshape.55.before_ref, s32[4,3072]{1,0:T(4,128)S(1)} %fusion.ids_ref, bf16[3072,128]{1,0:T(8,128)(2,1)S(1)} %get-tuple-element.88.refs_0_, bf16[3072,128]{1,0:T(8,128)(2,1)} %collective-permute-done.39.refs_1_, ...), custom_call_target="tpu_custom_call" | custom-call | flops 1073741824 | bytes 5242880 | tf_op jit(solution)/shard_map/fold/pallas_call | solution.py:413
  404.4 12.5 %collective-permute-done.54.refs_3_ = bf16[4096,128]{1,0:T(8,128)(2,1)S(1)} collective-permute-done((bf16[4096,128]{1,0:T(8,128)(2,1)S(1)}, bf16[4096,128]{1,0:T(8,128)(2,1)S(1)}, u32[]{:S(2)}, u32[]{:S(2)}) %collective-permute-start.54) | collective-permute-done | bytes 1048608 | tf_op jit(solution)/shard_map/ppermute | solution.py:314
  424.5 16.1 %collective-permute-done.61.refs_10_ = bf16[4096,128]{1,0:T(8,128)(2,1)} collective-permute-done((bf16[4096,128]{1,0:T(8,128)(2,1)S(1)}, bf16[4096,128]{1,0:T(8,128)(2,1)}, u32[]{:S(2)}, u32[]{:S(2)}) %collective-permute-start.61) | collective-permute-done | bytes 1048608 | tf_op jit(solution)/shard_map/ppermute | solution.py:314
  450.3 10.9 %collective-permute-done.58.refs_7_ = bf16[4096,128]{1,0:T(8,128)(2,1)} collective-permute-done((bf16[4096,128]{1,0:T(8,128)(2,1)S(1)}, bf16[4096,128]{1,0:T(8,128)(2,1)}, u32[]{:S(2)}, u32[]{:S(2)}) %collective-permute-start.58) | collective-permute-done | bytes 1048608 | tf_op jit(solution)/shard_map/ppermute | solution.py:314
  467.8 20.5 %collective-permute-done.62.refs_11_ = bf16[4096,128]{1,0:T(8,128)(2,1)S(1)} collective-permute-done((bf16[4096,128]{1,0:T(8,128)(2,1)S(1)}, bf16[4096,128]{1,0:T(8,128)(2,1)S(1)}, u32[]{:S(2)}, u32[]{:S(2)}) %collective-permute-start.62) | collective-permute-done | bytes 1048608 | tf_op jit(solution)/shard_map/ppermute | solution.py:314
  488.3 22.1 %collective-permute-done.59.refs_8_ = bf16[4096,128]{1,0:T(8,128)(2,1)} collective-permute-done((bf16[4096,128]{1,0:T(8,128)(2,1)S(1)}, bf16[4096,128]{1,0:T(8,128)(2,1)}, u32[]{:S(2)}, u32[]{:S(2)}) %collective-permute-start.59) | collective-permute-done | bytes 1048608 | tf_op jit(solution)/shard_map/ppermute | solution.py:314
  520.2 14.7 %curvature.1.curve_ref = f32[4096,1]{1,0:T(8,128)S(1)} custom-call(s32[288]{0:T(512)S(1)} %pad_add_fusion.lows_ref, s32[16,1,3072]{2,1,0:T(1,128)S(1)} %copy.39.ids_ref, f32[16,1,3072]{2,1,0:T(1,128)S(1)} %copy.40.nominal_ref, f32[4096,1]{1,0:T(8,128)S(1)} %copy.41.background_ref, f32[4096,1]{1,0:T(8,128)S(1)} %copy-done.10), custom_call_target="tpu_custom_call" | custom-call | tf_op jit(solution)/shard_map/curvature/pallas_call | solution.py:465
  545.7 27.5 %hessian.1 = (f32[384,3072]{1,0:T(8,128)}, bf16[384,3072]{1,0:T(8,128)(2,1)}) custom-call(bf16[384,4096]{1,0:T(8,128)(2,1)} %copy-done.18, bf16[4096,128]{1,0:T(8,128)(2,1)S(1)} %copy-done.13, bf16[4096,128]{1,0:T(8,128)(2,1)S(1)} %copy-done.15, bf16[4096,128]{1,0:T(8,128)(2,1)S(1)} %copy-done.17, bf16[4096,128]{1,0:T(8,128)(2,1)S(1)} %copy-done.25, ...), custom_call_target="tpu_custom_call" | custom-call | flops 9663676416 | bytes 25165824 | tf_op jit(solution)/shard_map/hessian/pallas_call | solution.py:549
  577.2 55.6 %sum_over_planes.1 = f32[96,3072]{1,0:T(8,128)S(1)} custom-call(f32[384,3072]{1,0:T(8,128)S(1)} %copy-done.11, bf16[384,3072]{1,0:T(8,128)(2,1)S(1)} %copy-done.19), custom_call_target="tpu_custom_call" | custom-call | tf_op jit(solution)/shard_map/sum_over_planes/pallas_call | solution.py:621
  (282 shorter events, 235.5 us)
Async XLA Ops:
  65.4 65.2 %collective-permute-start.18 = (s16[4096,128]{1,0:T(8,128)(2,1)}, s16[4096,128]{1,0:T(8,128)(2,1)}, u32[]{:S(2)}, u32[]{:S(2)}) collective-permute-start(s16[4096,128]{1,0:T(8,128)(2,1)} %get-tuple-element.51), channel_id=1, source_target_pairs={{24,16},{26,18},{28,20},{30,22},{25,17},{27,19},{29,21},{31,23}} | collective-permute-start | bytes 3145736 | tf_op jit(solution)/shard_map/ppermute | solution.py:314
  86.6 46.4 %collective-permute-start.12 = (s16[4096,128]{1,0:T(8,128)(2,1)}, s16[4096,128]{1,0:T(8,128)(2,1)}, u32[]{:S(2)}, u32[]{:S(2)}) collective-permute-start(s16[4096,128]{1,0:T(8,128)(2,1)} %get-tuple-element.45), channel_id=1, source_target_pairs={{0,8},{2,10},{4,12},{6,14},{1,9},{3,11},{5,13},{7,15}} | collective-permute-start | bytes 3145736 | tf_op jit(solution)/shard_map/ppermute | solution.py:314
  130.6 63.1 %collective-permute-start.33 = (s16[4096,128]{1,0:T(8,128)(2,1)}, s16[4096,128]{1,0:T(8,128)(2,1)}, u32[]{:S(2)}, u32[]{:S(2)}) collective-permute-start(s16[4096,128]{1,0:T(8,128)(2,1)} %get-tuple-element.64), channel_id=1, source_target_pairs={{24,16},{26,18},{28,20},{30,22},{25,17},{27,19},{29,21},{31,23}} | collective-permute-start | bytes 3145736 | tf_op jit(solution)/shard_map/ppermute | solution.py:314
  132.9 74.1 %collective-permute-start.27 = (s16[4096,128]{1,0:T(8,128)(2,1)}, s16[4096,128]{1,0:T(8,128)(2,1)}, u32[]{:S(2)}, u32[]{:S(2)}) collective-permute-start(s16[4096,128]{1,0:T(8,128)(2,1)} %get-tuple-element.58), channel_id=1, source_target_pairs={{0,8},{2,10},{4,12},{6,14},{1,9},{3,11},{5,13},{7,15}} | collective-permute-start | bytes 3145736 | tf_op jit(solution)/shard_map/ppermute | solution.py:314
  163.0 62.2 %collective-permute-start.20 = (s16[4096,128]{1,0:T(8,128)(2,1)}, s16[4096,128]{1,0:T(8,128)(2,1)}, u32[]{:S(2)}, u32[]{:S(2)}) collective-permute-start(s16[4096,128]{1,0:T(8,128)(2,1)} %get-tuple-element.53), channel_id=1, source_target_pairs={{16,8},{18,10},{20,12},{22,14},{24,16},{26,18},{28,20},{30,22},{17... | collective-permute-start | bytes 3145736 | tf_op jit(solution)/shard_map/ppermute | solution.py:314
  176.3 62.1 %collective-permute-start.14 = (s16[4096,128]{1,0:T(8,128)(2,1)}, s16[4096,128]{1,0:T(8,128)(2,1)}, u32[]{:S(2)}, u32[]{:S(2)}) collective-permute-start(s16[4096,128]{1,0:T(8,128)(2,1)} %get-tuple-element.47), channel_id=1, source_target_pairs={{0,8},{2,10},{4,12},{6,14},{8,16},{10,18},{12,20},{14,22},{1,9},{3... | collective-permute-start | bytes 3145736 | tf_op jit(solution)/shard_map/ppermute | solution.py:314
  188.4 70.6 %collective-permute-start.48 = (s16[4096,128]{1,0:T(8,128)(2,1)}, s16[4096,128]{1,0:T(8,128)(2,1)}, u32[]{:S(2)}, u32[]{:S(2)}) collective-permute-start(s16[4096,128]{1,0:T(8,128)(2,1)} %get-tuple-element.77), channel_id=1, source_target_pairs={{24,16},{26,18},{28,20},{30,22},{25,17},{27,19},{29,21},{31,23}} | collective-permute-start | bytes 3145736 | tf_op jit(solution)/shard_map/ppermute | solution.py:314
  193.8 79.5 %collective-permute-start.42 = (s16[4096,128]{1,0:T(8,128)(2,1)}, s16[4096,128]{1,0:T(8,128)(2,1)}, u32[]{:S(2)}, u32[]{:S(2)}) collective-permute-start(s16[4096,128]{1,0:T(8,128)(2,1)} %get-tuple-element.71), channel_id=1, source_target_pairs={{0,8},{2,10},{4,12},{6,14},{1,9},{3,11},{5,13},{7,15}} | collective-permute-start | bytes 3145736 | tf_op jit(solution)/shard_map/ppermute | solution.py:314
  215.5 86.7 %collective-permute-start.35 = (s16[4096,128]{1,0:T(8,128)(2,1)}, s16[4096,128]{1,0:T(8,128)(2,1)}, u32[]{:S(2)}, u32[]{:S(2)}) collective-permute-start(s16[4096,128]{1,0:T(8,128)(2,1)} %get-tuple-element.66), channel_id=1, source_target_pairs={{16,8},{18,10},{20,12},{22,14},{24,16},{26,18},{28,20},{30,22},{17... | collective-permute-start | bytes 3145736 | tf_op jit(solution)/shard_map/ppermute | solution.py:314
  236.8 77.9 %collective-permute-start.29 = (s16[4096,128]{1,0:T(8,128)(2,1)}, s16[4096,128]{1,0:T(8,128)(2,1)}, u32[]{:S(2)}, u32[]{:S(2)}) collective-permute-start(s16[4096,128]{1,0:T(8,128)(2,1)} %get-tuple-element.60), channel_id=1, source_target_pairs={{0,8},{2,10},{4,12},{6,14},{8,16},{10,18},{12,20},{14,22},{1,9},{3... | collective-permute-start | bytes 3145736 | tf_op jit(solution)/shard_map/ppermute | solution.py:314
  243.3 87.8 %collective-permute-start.22 = (s16[4096,128]{1,0:T(8,128)(2,1)}, s16[4096,128]{1,0:T(8,128)(2,1)}, u32[]{:S(2)}, u32[]{:S(2)}) collective-permute-start(s16[4096,128]{1,0:T(8,128)(2,1)} %get-tuple-element.55), channel_id=1, source_target_pairs={{8,0},{10,2},{12,4},{14,6},{16,8},{18,10},{20,12},{22,14},{24,16},... | collective-permute-start | bytes 3145736 | tf_op jit(solution)/shard_map/ppermute | solution.py:314
  271.9 60.6 %collective-permute-start.16 = (s16[4096,128]{1,0:T(8,128)(2,1)}, s16[4096,128]{1,0:T(8,128)(2,1)}, u32[]{:S(2)}, u32[]{:S(2)}) collective-permute-start(s16[4096,128]{1,0:T(8,128)(2,1)} %get-tuple-element.49), channel_id=1, source_target_pairs={{0,8},{2,10},{4,12},{6,14},{8,16},{10,18},{12,20},{14,22},{16,24},... | collective-permute-start | bytes 3145736 | tf_op jit(solution)/shard_map/ppermute | solution.py:314
  283.2 70.7 %collective-permute-start.50 = (s16[4096,128]{1,0:T(8,128)(2,1)}, s16[4096,128]{1,0:T(8,128)(2,1)}, u32[]{:S(2)}, u32[]{:S(2)}) collective-permute-start(s16[4096,128]{1,0:T(8,128)(2,1)} %get-tuple-element.79), channel_id=1, source_target_pairs={{16,8},{18,10},{20,12},{22,14},{24,16},{26,18},{28,20},{30,22},{17... | collective-permute-start | bytes 3145736 | tf_op jit(solution)/shard_map/ppermute | solution.py:314
  302.1 53.3 %collective-permute-start.44 = (s16[4096,128]{1,0:T(8,128)(2,1)}, s16[4096,128]{1,0:T(8,128)(2,1)}, u32[]{:S(2)}, u32[]{:S(2)}) collective-permute-start(s16[4096,128]{1,0:T(8,128)(2,1)} %get-tuple-element.73), channel_id=1, source_target_pairs={{0,8},{2,10},{4,12},{6,14},{8,16},{10,18},{12,20},{14,22},{1,9},{3... | collective-permute-start | bytes 3145736 | tf_op jit(solution)/shard_map/ppermute | solution.py:314
  320.6 48.9 %collective-permute-start.37 = (s16[4096,128]{1,0:T(8,128)(2,1)S(1)}, s16[4096,128]{1,0:T(8,128)(2,1)S(1)}, u32[]{:S(2)}, u32[]{:S(2)}) collective-permute-start(s16[4096,128]{1,0:T(8,128)(2,1)S(1)} %get-tuple-element.68), channel_id=1, source_target_pairs={{8,0},{10,2},{12,4},{14,6},{16,8},{18,10},{20,12},{22,14},{24,16},... | collective-permute-start | bytes 3145736 | tf_op jit(solution)/shard_map/ppermute | solution.py:314
  331.1 48.6 %collective-permute-start.31 = (s16[4096,128]{1,0:T(8,128)(2,1)S(1)}, s16[4096,128]{1,0:T(8,128)(2,1)S(1)}, u32[]{:S(2)}, u32[]{:S(2)}) collective-permute-start(s16[4096,128]{1,0:T(8,128)(2,1)S(1)} %get-tuple-element.62), channel_id=1, source_target_pairs={{0,8},{2,10},{4,12},{6,14},{8,16},{10,18},{12,20},{14,22},{16,24},... | collective-permute-start | bytes 3145736 | tf_op jit(solution)/shard_map/ppermute | solution.py:314
  354.0 45.6 %collective-permute-start.60 = (bf16[4096,128]{1,0:T(8,128)(2,1)S(1)}, bf16[4096,128]{1,0:T(8,128)(2,1)S(1)}, u32[]{:S(2)}, u32[]{:S(2)}) collective-permute-start(bf16[4096,128]{1,0:T(8,128)(2,1)S(1)} %fold_last.3.refs_0_), channel_id=1, source_target_pairs={{0,6},{2,4},{4,2},{6,0},{8,14},{10,12},{12,10},{14,8},{16,22},{18,... | collective-permute-start | bytes 3145736 | tf_op jit(solution)/shard_map/ppermute | solution.py:314
  355.4 47.5 %collective-permute-start.57 = (bf16[4096,128]{1,0:T(8,128)(2,1)S(1)}, bf16[4096,128]{1,0:T(8,128)(2,1)S(1)}, u32[]{:S(2)}, u32[]{:S(2)}) collective-permute-start(bf16[4096,128]{1,0:T(8,128)(2,1)S(1)} %fold_last.3.refs_0_), channel_id=1, source_target_pairs={{0,4},{2,6},{4,0},{6,2},{8,12},{10,14},{12,8},{14,10},{16,20},{18,... | collective-permute-start | bytes 3145736 | tf_op jit(solution)/shard_map/ppermute | solution.py:314
  416.9 44.4 %collective-permute-start.58 = (bf16[4096,128]{1,0:T(8,128)(2,1)S(1)}, bf16[4096,128]{1,0:T(8,128)(2,1)}, u32[]{:S(2)}, u32[]{:S(2)}) collective-permute-start(bf16[4096,128]{1,0:T(8,128)(2,1)S(1)} %fold_last.4.refs_1_), channel_id=1, source_target_pairs={{0,4},{2,6},{4,0},{6,2},{8,12},{10,14},{12,8},{14,10},{16,20},{18,... | collective-permute-start | bytes 3145736 | tf_op jit(solution)/shard_map/ppermute | solution.py:314
  462.9 47.5 %collective-permute-start.59 = (bf16[4096,128]{1,0:T(8,128)(2,1)S(1)}, bf16[4096,128]{1,0:T(8,128)(2,1)}, u32[]{:S(2)}, u32[]{:S(2)}) collective-permute-start(bf16[4096,128]{1,0:T(8,128)(2,1)S(1)} %fold_last.5.refs_2_), channel_id=1, source_target_pairs={{0,4},{2,6},{4,0},{6,2},{8,12},{10,14},{12,8},{14,10},{16,20},{18,... | collective-permute-start | bytes 3145736 | tf_op jit(solution)/shard_map/ppermute | solution.py:314
  463.9 46.5 %collective-permute-start.56 = (bf16[4096,128]{1,0:T(8,128)(2,1)S(1)}, bf16[4096,128]{1,0:T(8,128)(2,1)}, u32[]{:S(2)}, u32[]{:S(2)}) collective-permute-start(bf16[4096,128]{1,0:T(8,128)(2,1)S(1)} %fold_last.5.refs_2_), channel_id=1, source_target_pairs={{0,2},{2,0},{4,6},{6,4},{8,10},{10,8},{12,14},{14,12},{16,18},{18,... | collective-permute-start | bytes 3145736 | tf_op jit(solution)/shard_map/ppermute | solution.py:314
  466.9 44.0 %collective-permute-start.73 = (bf16[4096,128]{1,0:T(8,128)(2,1)}, bf16[4096,128]{1,0:T(8,128)(2,1)}, u32[]{:S(2)}, u32[]{:S(2)}) collective-permute-start(bf16[4096,128]{1,0:T(8,128)(2,1)} %collective-permute-done.61.refs_10_), channel_id=1, source_target_pairs={{0,1},{1,0},{2,3},{3,2},{4,5},{5,4},{6,7},{7,6},{8,9},{9,8},{10,11... | collective-permute-start | bytes 3145736 | tf_op jit(solution)/shard_map/ppermute | solution.py:18
  467.2 78.4 %collective-permute-start.70 = (bf16[4096,128]{1,0:T(8,128)(2,1)}, bf16[4096,128]{1,0:T(8,128)(2,1)}, u32[]{:S(2)}, u32[]{:S(2)}) collective-permute-start(bf16[4096,128]{1,0:T(8,128)(2,1)} %collective-permute-done.58.refs_7_), channel_id=1, source_target_pairs={{0,1},{1,0},{2,3},{3,2},{4,5},{5,4},{6,7},{7,6},{8,9},{9,8},{10,11... | collective-permute-start | bytes 3145736 | tf_op jit(solution)/shard_map/ppermute | solution.py:18
  488.3 57.4 %collective-permute-start.67 = (bf16[4096,128]{1,0:T(8,128)(2,1)}, bf16[4096,128]{1,0:T(8,128)(2,1)}, u32[]{:S(2)}, u32[]{:S(2)}) collective-permute-start(bf16[4096,128]{1,0:T(8,128)(2,1)} %collective-permute-done.55.refs_4_), channel_id=1, source_target_pairs={{0,1},{1,0},{2,3},{3,2},{4,5},{5,4},{6,7},{7,6},{8,9},{9,8},{10,11... | collective-permute-start | bytes 3145736 | tf_op jit(solution)/shard_map/ppermute | solution.py:18
  (94 other events, 1835.9 us)

commit v2 on v1

--- a/solution.py
+++ b/solution.py
@@ -327,108 +327,327 @@
     return rows == lax.broadcasted_iota(jnp.int32, (LANES, LANES), 1)
 
 
-def fold_kernel(sources, steps, received, last, info_ref, before_ref, ids_ref, *refs):
-    rows_refs = refs[:sources]
-    got = refs[sources : sources + 2 * received]
-    outs = refs[sources + 2 * received : -1]
-    acc = refs[-1]
-    events = ids_ref.shape[1]
-    block = outs[0].shape[0]
-    tiles = block // TILE
-    bounds = before_ref.shape[0] // sources
-
-    @pl.when(info_ref[1] == 1)
+def slots_kernel(bins_dev, starts_ref, table_ref, out_ref):
+    owners, sources, slot = out_ref.shape
+    events = table_ref.shape[1]
+    table = table_ref[...]
+
+    @pl.loop(0, owners)
+    def _(o):
+        for s in range(sources):
+            start = starts_ref[s * owners + o] * 16
+            turned = pltpu.roll(table, lax.rem(events - start, events), axis=1)[s : s + 1, :slot]
+            bins = turned - (o * bins_dev).astype(jnp.float32)
+            inside = (bins >= 0) & (bins < bins_dev)
+            out_ref[o, s : s + 1, :] = jnp.where(inside, bins, -1.0)
+
+
+def slots_of(starts, ids, owners, slot, bins_dev):
+    sources, events = ids.shape
+    table = jnp.concatenate([ids, jnp.zeros((8 - sources, events), jnp.float32)])
+    return pl.pallas_call(
+        functools.partial(slots_kernel, bins_dev),
+        out_shape=jax.ShapeDtypeStruct((owners, sources, slot), jnp.float32),
+        in_specs=[
+            pl.BlockSpec(memory_space=pltpu.SMEM),
+            pl.BlockSpec(memory_space=pltpu.VMEM),
+        ],
+        out_specs=pl.BlockSpec(memory_space=pltpu.VMEM),
+        name="slots",
+    )(starts, table)
+
+
+def chain_kernel(near, far, chunks, pieces, slot, starts_ref, local_ref, weights_ref, *refs):
+    firsts = refs[:near]
+    out_ref = refs[near]
+    rows_refs = refs[near + 1 : near + 1 + chunks]
+    (
+        window, acc, own, send_q, send_s, got_q, got_s,
+        row_sem, row_send, row_recv, q_send, q_recv, s_send, s_recv,
+        own_sem, side_send, side_recv, pair_send, pair_recv,
+    ) = refs[near + 1 + chunks :]
+    owners = near * far
+    here = lax.axis_index("bins")
+    core = lax.axis_index("params")
+    z, me = here // near, lax.rem(here, near)
+    bins_dev = own.shape[1] // near
+    width = chunks * LANES
+    held = near // pieces
+    size = held * bins_dev
+    lines = size // LANES
+
+    def side(d):
+        return z * near + xor_of(me, d, near)
+
+    def along(way):
+        return (z + 1 - 2 * way) * near + me
+
+    barrier = pltpu.get_barrier_semaphore()
+    for d in range(1, near):
+        pl.semaphore_signal(barrier, inc=1, device_id={"bins": side(d)}, device_id_type=MESH)
+    pl.semaphore_signal(barrier, inc=1, device_id={"params": 1 - core}, device_id_type=MESH)
+
+    @pl.when(z < far - 1)
     def _():
-        @pl.loop(0, tiles)
-        def _(k):
-            index = (info_ref[0] * steps + pl.program_id(0)) * tiles + k
-            bins = index * TILE + lax.broadcasted_iota(jnp.int32, (TILE, LANES), 0)
-
-            def product(s, start):
-                ids = ids_ref[s : s + 1, pl.ds(start, LANES)]
-                hot = (bins == ids).astype(jnp.bfloat16)
-                return jnp.dot(
-                    hot, rows_refs[s][pl.ds(start, LANES), :], preferred_element_type=jnp.float32
-                )
-
-            total = jnp.zeros((TILE, LANES), jnp.float32)
-            firsts = []
-            for s in range(sources):
-                low = before_ref[s * bounds + index]
-                first = jnp.minimum(low // LANES * LANES, events - 2 * LANES)
-                first = pl.multiple_of(first, LANES)
-                firsts.append(first)
-                total += product(s, first)
-                total += product(s, pl.multiple_of(first + LANES, LANES))
-            acc[...] = total
-            for s in range(sources):
-                high = before_ref[s * bounds + index + 1]
-                rest = jnp.maximum(high - firsts[s] - 2 * LANES + LANES - 1, 0) // LANES
-                begin = firsts[s] + 2 * LANES
-
-                @pl.loop(0, rest)
-                def _(e):
-                    acc[...] += product(s, pl.multiple_of(begin + e * LANES, LANES))
-
-            eye = diagonal()
-            for h in range(TILE // LANES):
-                line = k * (TILE // LANES) + h
-                part = pl.ds(pl.multiple_of(line * LANES, LANES), LANES)
-                value = acc[h * LANES : (h + 1) * LANES, :]
-                for n in range(received):
-                    scale = got[2 * n + 1][pl.ds(line, 1), :]
-                    scale = jnp.sum(jnp.where(eye, scale, 0.0), axis=1, keepdims=True)
-                    value += got[2 * n][part, :].astype(jnp.int32).astype(jnp.float32) * scale
-                if last:
-                    outs[0][part, :] = value.astype(outs[0].dtype)
-                else:
-                    most = jnp.max(jnp.abs(value), axis=1, keepdims=True)
-                    wide = most * (2.0**23 + 1.0)
-                    step = (wide + (most - wide)) * 2.0**-14
-                    factor = jnp.where(most > 1e-30, 1.0 / step, 0.0)
-                    coded = jnp.round(value * factor).astype(jnp.int32)
-                    outs[0][part, :] = coded.astype(outs[0].dtype)
-                    scale = jnp.where(eye, step, 0.0)
-                    outs[1][pl.ds(line, 1), :] = jnp.sum(scale, axis=0, keepdims=True)
-
-
-def fold(info, before, ids, rows, got, bins, last):
-    sources, events = ids.shape
-    block = 8 * LANES
-    steps = bins // block
-    smem = pl.BlockSpec(memory_space=pltpu.SMEM)
-    values = pl.BlockSpec((block, LANES), lambda j: (j, 0))
-    scales = pl.BlockSpec((8, LANES), lambda j: (j, 0))
-    whole_rows = pl.BlockSpec((events, LANES), lambda j: (0, 0))
-    flat = [part for pair in got for part in pair]
-    if last:
-        out_shape = [jax.ShapeDtypeStruct((bins, LANES), jnp.bfloat16)]
-        out_specs = [values]
-    else:
-        out_shape = [
-            jax.ShapeDtypeStruct((bins, LANES), jnp.int16),
-            jax.ShapeDtypeStruct((bins // LANES, LANES), jnp.float32),
+        pl.semaphore_signal(barrier, inc=1, device_id={"bins": along(0)}, device_id_type=MESH)
+
+    @pl.when(z > 0)
+    def _():
+        pl.semaphore_signal(barrier, inc=1, device_id={"bins": along(1)}, device_id_type=MESH)
+
+    inner = (z > 0).astype(jnp.int32) + (z < far - 1).astype(jnp.int32)
+    pl.semaphore_wait(barrier, near + inner)
+
+    def quarter(d, c):
+        start = xor_of(me, d, near) * width + c * LANES
+        return weights_ref.at[:, pl.ds(pl.multiple_of(start, LANES), LANES)]
+
+    def row_copy(c, d):
+        return pltpu.make_async_remote_copy(
+            src_ref=quarter(d, c),
+            dst_ref=rows_refs[c].at[d],
+            send_sem=row_send.at[c, d],
+            recv_sem=row_recv.at[c, d],
+            device_id={"bins": side(d)},
+            device_id_type=MESH,
+        )
+
+    def row_local(c, d):
+        source = firsts[d] if c == 0 else quarter(d, c)
+        return pltpu.make_async_copy(source, rows_refs[c].at[d], row_sem.at[c, d])
+
+    for d in range(near):
+        row_local(0, d).start()
+    for c in range(1, chunks):
+        row_local(c, 0).start()
+        for d in range(1, near):
+            row_copy(c, d).start()
+
+    def chain_copies(way, c, r, p):
+        return [
+            pltpu.make_async_remote_copy(
+                src_ref=source.at[way, c, r - 1, p],
+                dst_ref=target.at[way, c, r - 1, p],
+                send_sem=sent.at[way, c, r - 1, p],
+                recv_sem=landed.at[way, c, r - 1, p],
+                device_id={"bins": along(way)},
+                device_id_type=MESH,
+            )
+            for source, target, sent, landed in (
+                (send_q, got_q, q_send, q_recv), (send_s, got_s, s_send, s_recv)
+            )
         ]
-        out_specs = [values, scales]
+
+    def fold(c, plane, p, inputs, finish):
+        @pl.loop(0, held)
+        def _(i):
+            owner = plane * near + p * held + i
+            for s in range(near):
+                start = starts_ref[s * owners + owner] * 16
+                window[s * slot : (s + 1) * slot, :] = rows_refs[c][s, pl.ds(start, slot), :]
+
+            @pl.loop(0, bins_dev // TILE)
+            def _(k):
+                bins = k * TILE + lax.broadcasted_iota(jnp.int32, (TILE, near * slot), 0)
+                hot = (bins == local_ref[owner]).astype(jnp.bfloat16)
+                acc[...] = jnp.dot(hot, window[...], preferred_element_type=jnp.float32)
+                base = i * (bins_dev // LANES) + k * (TILE // LANES)
+                eye = diagonal()
+                for way, r, has in inputs:
+                    @pl.when(has)
+                    def _():
+                        for h in range(TILE // LANES):
+                            line = base + h
+                            part = pl.ds(pl.multiple_of(line * LANES, LANES), LANES)
+                            step = got_s[way, c, r - 1, p, pl.ds(line, 1), :]
+                            step = jnp.sum(jnp.where(eye, step, 0.0), axis=1, keepdims=True)
+                            coded = got_q[way, c, r - 1, p, part, :].astype(jnp.int32)
+                            acc[h * LANES : (h + 1) * LANES, :] += (
+                                coded.astype(jnp.float32) * step
+                            )
+                for h in range(TILE // LANES):
+                    line = base + h
+                    part = pl.ds(pl.multiple_of(line * LANES, LANES), LANES)
+                    finish(acc[h * LANES : (h + 1) * LANES, :], line, part, eye)
+
+    def wait_chain(way, c, r, p):
+        for copy in chain_copies(way, c, r, p):
+            copy.wait_recv()
+
+    def rounds(c, first, last):
+        @pl.loop(first, last)
+        def _(r):
+            @pl.loop(0, pieces)
+            def _(p):
+                for way in range(2):
+                    step_in = z if way == 0 else far - 1 - z
+
+                    @pl.when(step_in < r)
+                    def _():
+                        has = step_in > 0
+
+                        @pl.when(has)
+                        def _():
+                            wait_chain(way, c, r - 1, p)
+
+                        def code(value, line, part, eye):
+                            most = jnp.max(jnp.abs(value), axis=1, keepdims=True)
+                            wide = most * (2.0**23 + 1.0)
+                            step = (wide + (most - wide)) * 2.0**-14
+                            factor = jnp.where(most > 1e-30, 1.0 / step, 0.0)
+                            coded = jnp.round(value * factor).astype(jnp.int32)
+                            send_q[way, c, r - 1, p, part, :] = coded.astype(send_q.dtype)
+                            send_s[way, c, r - 1, p, pl.ds(line, 1), :] = jnp.sum(
+                                jnp.where(eye, step, 0.0), axis=0, keepdims=True
+                            )
+
+                        plane = z + (far - r) * (1 - 2 * way)
+                        fold(c, plane, p, [(way, r - 1, has)], code)
+                        for copy in chain_copies(way, c, r, p):
+                            copy.start()
+
+    def rows_part(p):
+        return pl.ds(pl.multiple_of(p * size, size), size)
+
+    def side_copy(c, d, p):
+        return pltpu.make_async_remote_copy(
+            src_ref=own.at[c, rows_part(p), :],
+            dst_ref=out_ref.at[0, d, c, rows_part(p), :],
+            send_sem=side_send.at[c, d, p],
+            recv_sem=side_recv.at[c, d, p],
+            device_id={"bins": side(d)},
+            device_id_type=MESH,
+        )
+
+    def pair_copy(c, d, p):
+        source = own.at[c] if d == 0 else out_ref.at[0, d, c]
+        return pltpu.make_async_remote_copy(
+            src_ref=source.at[rows_part(p), :],
+            dst_ref=out_ref.at[1, d, c, rows_part(p), :],
+            send_sem=pair_send.at[c, d, p],
+            recv_sem=pair_recv.at[c, d, p],
+            device_id={"params": 1 - core},
+            device_id_type=MESH,
+        )
+
+    def keep_copy(c, p):
+        return pltpu.make_async_copy(
+            own.at[c, rows_part(p), :], out_ref.at[0, 0, c, rows_part(p), :], own_sem.at[c, p]
+        )
+
+    def finish(c):
+        @pl.loop(0, pieces)
+        def _(p):
+            @pl.when(z > 0)
+            def _():
+                wait_chain(0, c, far - 1, p)
+
+            @pl.when(z < far - 1)
+            def _():
+                wait_chain(1, c, far - 1, p)
+
+            def store(value, line, part, eye):
+                row = pl.ds(pl.multiple_of(p * size + line * LANES, LANES), LANES)
+                own[c, row, :] = value.astype(own.dtype)
+
+            fold(c, z, p, [(0, far - 1, z > 0), (1, far - 1, z < far - 1)], store)
+            for d in range(1, near):
+                side_copy(c, d, p).start()
+            pair_copy(c, 0, p).start()
+            keep_copy(c, p).start()
+
+    def relay(c):
+        @pl.loop(0, pieces)
+        def _(p):
+            for d in range(1, near):
+                side_copy(c, d, p).wait_recv()
+                pair_copy(c, d, p).start()
+
+    for c in range(chunks):
+        row_local(c, 0).wait()
+        for d in range(1, near):
+            if c == 0:
+                row_local(c, d).wait()
+            else:
+                row_copy(c, d).wait_recv()
+        rounds(c, 1, 2)
+        if c > 0:
+            finish(c - 1)
+        rounds(c, 2, far)
+        if 0 < c < chunks - 1:
+            relay(c - 1)
+    finish(chunks - 1)
+    for c in range(max(chunks - 2, 0), chunks):
+        relay(c)
+
+    for c in range(chunks):
+        if c > 0:
+            for d in range(1, near):
+                row_copy(c, d).wait_send()
+
+        @pl.loop(0, pieces)
+        def _(p):
+            keep_copy(c, p).wait()
+            for d in range(1, near):
+                side_copy(c, d, p).wait_send()
+            for d in range(near):
+                pair_copy(c, d, p).wait_send()
+                pair_copy(c, d, p).wait_recv()
+
+            @pl.loop(1, far)
+            def _(r):
+                for way in range(2):
+                    step_in = z if way == 0 else far - 1 - z
+
+                    @pl.when(step_in < r)
+                    def _():
+                        for copy in chain_copies(way, c, r, p):
+                            copy.wait_send()
+
+
+def chain(starts, local, weights, firsts, near, far, chunks, slot, bins_dev):
+    events = weights.shape[0]
+    pieces = 2
+    bins = near * bins_dev
+    size = bins // pieces
+    hops = (2, chunks, far - 1, pieces)
+    dma = pltpu.SemaphoreType.DMA
     return pl.pallas_call(
-        functools.partial(fold_kernel, sources, steps, len(got), last),
-        grid=(steps,),
-        out_shape=out_shape,
-        in_specs=[smem, smem, pl.BlockSpec((sources, events), lambda j: (0, 0))]
-        + [whole_rows] * sources
-        + [values, scales] * len(got),
-        out_specs=out_specs,
-        scratch_shapes=[pltpu.VMEM((TILE, LANES), jnp.float32)],
+        functools.partial(chain_kernel, near, far, chunks, pieces, slot),
+        out_shape=jax.ShapeDtypeStruct((2, near, chunks, bins, LANES), jnp.bfloat16),
+        in_specs=[
+            pl.BlockSpec(memory_space=pltpu.SMEM),
+            pl.BlockSpec(memory_space=pltpu.VMEM),
+        ]
+        + [pl.BlockSpec(memory_space=pl.ANY)] * (1 + near),
+        out_specs=pl.BlockSpec(memory_space=pl.ANY),
+        scratch_shapes=[pltpu.VMEM((near, events, LANES), jnp.bfloat16)] * chunks
+        + [
+            pltpu.VMEM((near * slot, LANES), jnp.bfloat16),
+            pltpu.VMEM((TILE, LANES), jnp.float32),
+            pltpu.VMEM((chunks, bins, LANES), jnp.bfloat16),
+            pltpu.VMEM(hops + (size, LANES), jnp.int16),
+            pltpu.VMEM(hops + (size // LANES, LANES), jnp.float32),
+            pltpu.VMEM(hops + (size, LANES), jnp.int16),
+            pltpu.VMEM(hops + (size // LANES, LANES), jnp.float32),
+            dma((chunks, near)),
+            dma((chunks, near)),
+            dma((chunks, near)),
+            dma(hops),
+            dma(hops),
+            dma(hops),
+            dma(hops),
+            dma((chunks, pieces)),
+            dma((chunks, near, pieces)),
+            dma((chunks, near, pieces)),
+            dma((chunks, near, pieces)),
+            dma((chunks, near, pieces)),
+        ],
         compiler_params=pltpu.CompilerParams(
-            vmem_limit_bytes=24 << 20, dimension_semantics=("arbitrary",)
+            collective_id=3, has_side_effects=True, vmem_limit_bytes=60 << 20
         ),
-        cost_estimate=pl.CostEstimate(
-            flops=bins * 2 * sources * 256 * LANES,
-            bytes_accessed=2 * sources * events * LANES + 4 * bins * LANES,
-            transcendentals=0,
-        ),
-        name="fold_last" if last else "fold",
-    )(info, before, ids, *rows, *flat)
+        name="chain",
+    )(starts, local, weights, *firsts)
 
 
 def curve_kernel(lows_ref, ids_ref, nominal_ref, background_ref, observed_ref, out_ref, acc):
@@ -482,15 +701,15 @@
     )
 
 
-def weigh_kernel(near, chunks, piece, me_ref, curve_ref, *refs):
-    out_ref = refs[-1]
+def weigh_kernel(piece, me_ref, curve_ref, templates_ref, out_ref):
+    _, near, chunks, _, _ = templates_ref.shape
     rows = lax.broadcasted_iota(jnp.int32, (piece, LANES), 0) + me_ref[0] * piece
     lanes = lax.broadcasted_iota(jnp.int32, (piece, LANES), 1)
     for d in range(near):
         total = 0.0
         for c in range(chunks):
             pick = (rows == lanes + c * LANES).astype(jnp.bfloat16)
-            value = curve_ref[...] * refs[d * chunks + c][...].astype(jnp.float32)
+            value = curve_ref[...] * templates_ref[0, d, c].astype(jnp.float32)
             total += lax.dot_general(
                 pick, value.astype(jnp.bfloat16), (((1,), (1,)), ((), ())),
                 preferred_element_type=jnp.float32,
@@ -498,40 +717,38 @@
         out_ref[d * piece : (d + 1) * piece, :] = total.astype(out_ref.dtype)
 
 
-def weigh(me, curve, templates, near, chunks, piece):
-    bins = curve.shape[0]
+def weigh(me, curve, templates, piece):
+    _, near, chunks, bins, _ = templates.shape
     tile = 512
     return pl.pallas_call(
-        functools.partial(weigh_kernel, near, chunks, piece),
+        functools.partial(weigh_kernel, piece),
         grid=(bins // tile,),
         out_shape=jax.ShapeDtypeStruct((near * piece, bins), jnp.bfloat16),
         in_specs=[
             pl.BlockSpec(memory_space=pltpu.SMEM),
             pl.BlockSpec((tile, 1), lambda j: (j, 0)),
-        ]
-        + [pl.BlockSpec((tile, LANES), lambda j: (j, 0))] * (near * chunks),
+            pl.BlockSpec((1, near, chunks, tile, LANES), lambda j: (0, 0, 0, j, 0)),
+        ],
         out_specs=pl.BlockSpec((near * piece, tile), lambda j: (0, j)),
         compiler_params=pltpu.CompilerParams(
             vmem_limit_bytes=24 << 20, dimension_semantics=("arbitrary",)
         ),
         name="weigh",
-    )(me, curve, *templates)
-
-
-def hessian_kernel(count, weighted_ref, *refs):
-    pieces = refs[:count]
-    full_ref, coded_ref, held, sems = refs[count:]
-    bins = held.shape[0]
-    depth = math.gcd(bins, 1024)
+    )(me, curve, templates)
+
+
+def hessian_kernel(weighted_ref, templates_ref, full_ref, coded_ref, held, sems):
+    groups, near, chunks, _, _ = templates_ref.shape
+    places = [(k, d, c) for k in range(groups) for d in range(near) for c in range(chunks)]
 
     def fetch(n):
         return pltpu.make_async_copy(
-            pieces[n], held.at[:, n * LANES : (n + 1) * LANES], sems.at[n]
-        )
-
-    for n in range(count):
+            templates_ref.at[places[n]], held.at[:, n * LANES : (n + 1) * LANES], sems.at[n]
+        )
+
+    for n in range(len(places)):
         fetch(n).start()
-    for n in range(0, count, 2):
+    for n in range(0, len(places), 2):
         fetch(n).wait()
         fetch(n + 1).wait()
         columns = slice(n * LANES, (n + 2) * LANES)
@@ -542,18 +759,17 @@
         coded_ref[:, columns] = total.astype(coded_ref.dtype)
 
 
-def hessian_of(weighted, pieces):
+def hessian_of(weighted, templates):
     rows, bins = weighted.shape
-    count = len(pieces)
+    count = math.prod(templates.shape[:3])
     shape = (rows, count * LANES)
     return pl.pallas_call(
-        functools.partial(hessian_kernel, count),
+        hessian_kernel,
         out_shape=[
             jax.ShapeDtypeStruct(shape, jnp.float32),
             jax.ShapeDtypeStruct(shape, jnp.bfloat16),
         ],
-        in_specs=[pl.BlockSpec(memory_space=pltpu.VMEM)]
-        + [pl.BlockSpec(memory_space=pl.ANY)] * count,
+        in_specs=[pl.BlockSpec(memory_space=pltpu.VMEM), pl.BlockSpec(memory_space=pl.ANY)],
         out_specs=[pl.BlockSpec(memory_space=pltpu.VMEM)] * 2,
         scratch_shapes=[
             pltpu.VMEM((bins, count * LANES), jnp.bfloat16),
@@ -566,7 +782,7 @@
             transcendentals=0,
         ),
         name="hessian",
-    )(weighted, *pieces)
+    )(weighted, templates)
 
 
 def sum_kernel(near, far, piece, run, full_ref, coded_ref, out_ref, own, got, own_sem, sends, recvs):
@@ -646,9 +862,10 @@
     width = event_weights.shape[1] // near
     chunks = width // LANES
     bins = near * bins_dev
+    capacity = 3 * events // (2 * owners)
+    slot = -(-capacity // 16) * 16 + 16
     here = lax.axis_index("bins")
     z, me = here // near, lax.rem(here, near)
-    planes = range(far)
     around = [[(s, s // near * near + (s % near ^ d)) for s in range(owners)] for d in range(near)]
 
     def spread(value):
@@ -657,50 +874,17 @@
     meta = jnp.concatenate([event_bins.astype(jnp.float32), nominal.astype(jnp.float32)])
     meta = jnp.stack(spread(meta.reshape(2, events)))
     local = jnp.stack(spread(jnp.stack([background, observed])))
-    ids = meta[:, 0].astype(jnp.int32)
-    marks = jnp.arange(far * bins // TILE + 1, dtype=jnp.int32) * TILE
+    ids = meta[:, 0]
+    marks = (jnp.arange(owners, dtype=jnp.int32) * bins_dev).astype(jnp.float32)
     before = jnp.sum((ids[:, None, :] < marks[None, :, None]).astype(jnp.int32), axis=2)
-    before = before.reshape(-1)
-
-    def chunk_of(weights, c):
-        parts = []
-        for d in range(near):
-            start = (me ^ d) * width + c * LANES
-            part = lax.dynamic_slice(weights, (0, start), (events, LANES))
-            parts.append(part if d == 0 else shift(part, around[d]))
-        return parts
-
-    def info(target):
-        valid = (target >= 0) & (target < far)
-        return jnp.stack([jnp.clip(target, 0, far - 1), valid.astype(jnp.int32)])
-
-    def up(r):
-        return [(p * near + m, (p + 1) * near + m) for p in planes if p < r for m in range(near)]
-
-    def down(r):
-        return [
-            (p * near + m, (p - 1) * near + m) for p in planes if p >= far - r for m in range(near)
-        ]
-
-    def send(pair, pairs):
-        return tuple(shift(part, pairs) for part in pair)
-
-    rows_of = []
-    weights = event_weights
-    for c in range(chunks):
-        rows_of.append(chunk_of(weights, c))
-        weights, _ = lax.optimization_barrier((weights, rows_of[c][1:]))
-
-    own = [None] * chunks
-    for c in range(chunks):
-        rows = rows_of[c]
-        rising, falling = [], []
-        for r in range(1, far):
-            rising = [send(fold(info(z + far - r), before, ids, rows, rising, bins, False), up(r))]
-            falling = [
-                send(fold(info(z - far + r), before, ids, rows, falling, bins, False), down(r))
-            ]
-        own[c] = fold(info(z), before, ids, rows, rising + falling, bins, True)[0]
+    starts = jnp.minimum(before // 16, (events - slot) // 16).reshape(-1)
+    places = slots_of(starts, ids, owners, slot, bins_dev)
+    places = places.astype(jnp.int32).reshape(owners, 1, near * slot)
+
+    firsts = []
+    for d in range(near):
+        part = lax.dynamic_slice(event_weights, (0, (me ^ d) * width), (events, LANES))
+        firsts.append(part if d == 0 else shift(part, around[d]))
 
     metas = [meta] + [
         shift(meta, [(s, (s + k * near) % owners) for s in range(owners)]) for k in range(1, far)
@@ -710,20 +894,17 @@
     first_bin = z * bins
     near_marks = first_bin + jnp.arange(bins // TILE + 1, dtype=jnp.int32) * TILE
     lows = jnp.sum((all_ids[:, None, :] < near_marks[None, :, None]).astype(jnp.int32), axis=2)
-    places = jnp.arange(near, dtype=jnp.int32)
-    match = (places[None, :] ^ me) == places[:, None]
+    index = jnp.arange(near, dtype=jnp.int32)
+    match = (index[None, :] ^ me) == index[:, None]
     local = jnp.sum(jnp.where(match[:, :, None, None], local[None], 0.0), axis=1)
     curve = curvature_of(
         lows, first_bin, all_ids, metas[:, 1], local[:, 0].reshape(-1), local[:, 1].reshape(-1)
     )
 
-    mine = [spread(own[c]) for c in range(chunks)]
-    mine = [mine[c][d] for d in range(near) for c in range(chunks)]
-    theirs = [from_behind(part, "params", 1) for part in mine]
-    weighted = weigh(
-        me.reshape(1).astype(jnp.int32), curve, mine, near, chunks, width // far
-    )
-    full, coded = hessian_of(weighted, mine + theirs)
+    starts, curve = lax.optimization_barrier((starts, curve))
+    templates = chain(starts, places, event_weights, firsts, near, far, chunks, slot, bins_dev)
+    weighted = weigh(me.reshape(1).astype(jnp.int32), curve, templates, width // far)
+    full, coded = hessian_of(weighted, templates)
     summed = sum_over_planes(full, coded, near, far, width)
     return summed * (1.0 / (bins_dev * owners))
 

time: 636 us -> 411 us (0.65)
  waiting for transfers between devices: 193 us -> 0.03 us
  starting transfers between devices: 143 us -> 14.7 us
  Pallas kernels: 261 us -> 364 us
  local copies, waits for them, and re-layouts: 31.4 us -> 23.6 us
    ppermute x63 -> x12, waiting for transfers between devices: 193 us -> 0.03 us  [shift(): return lax.ppermute(value, 'bins', pairs)]
    ppermute x63 -> x12, starting transfers between devices: 141 us -> 14.7 us  [shift(): return lax.ppermute(value, 'bins', pairs)]
    pallas_call x23 -> x4, Pallas kernels: 191 us -> 279 us  [the longest x1 241 us: chain(): pl.pallas_call(functools.partial(chain_kernel, near, far, chunks, pieces,...]
    pallas_call x1, Pallas kernels: 55.6 us -> 70.5 us  [sum_over_planes(): pl.pallas_call(functools.partial(sum_kernel, near, far, piece, run), out_...]
    dynamic_slice x3 -> x1, local copies, waits for them, and re-layouts: 10 us -> 3.42 us  [body_by_parameters(): lax.dynamic_slice(event_weights, (0, (me ^ d) * width), (events, LANES))]
    unnamed x86 -> x8, local copies, waits for them, and re-layouts: 14.8 us -> 13.7 us
  transfers between devices with their start and end apart: 75 -> 12, of which waited for: 17 -> 0; matrix products, arithmetic and copies ran while one was open for 2% -> 3% of each run, Pallas kernels for 28% -> 5%
where the time goes in v2:
time: 411 us; the launch traced here: 409 us
  Pallas kernels  364 us (89%)
  local copies, waits for them, and re-layouts  23.6 us (6%)
  starting transfers between devices  14.7 us (4%)
  other arithmetic  5.96 us (1%)
    pallas_call x1, Pallas kernels, chain(): pl.pallas_call(functools.partial(chain_kernel, near, far, chunks, pieces,...  241 us
    pallas_call x1, Pallas kernels, sum_over_planes(): pl.pallas_call(functools.partial(sum_kernel, near, far, piece, run), out_...  70.5 us
    pallas_call x1, Pallas kernels, hessian_of(): pl.pallas_call(hessian_kernel, out_shape=[jax.ShapeDtypeStruct(shape, jnp...  25.2 us
    pallas_call x1, Pallas kernels, curvature_of(): pl.pallas_call(curve_kernel, grid=(bins // TILE,), out_shape=jax.ShapeDty...  14.7 us
    ppermute x12, starting transfers between devices, shift(): return lax.ppermute(value, 'bins', pairs)  14.7 us
    unnamed x8, local copies, waits for them, and re-layouts  13.7 us
  transfers between devices with their start and end apart: 12, of which 0 were waited for; matrix products, arithmetic and copies ran while one was open for 3% of the time, Pallas kernels for 5%

profile of v2, /device:TPU:28, one launch (start us, length us, event | category | flops | bytes accessed | tf_op | source)
XLA Modules:
  0.0 408.5 jit_solution(10360487071489341164)
XLA Ops:
  0.0 0.7 fusion.1
  1.3 1.5 collective-permute-start.6
  2.8 1.5 collective-permute-start.8
  5.7 1.5 collective-permute-start.2
  7.2 1.5 collective-permute-start.1
  8.8 3.4 constant_dynamic-slice_fusion
  12.8 1.5 collective-permute-start.11
  14.4 1.6 collective-permute-start.10
  16.2 2.0 copy.41.background_ref
  18.2 2.0 copy.42.observed_ref
  21.2 3.0 collective-permute-start.3
  25.8 4.6 %slots.1 = f32[16,4,304]{2,1,0:T(4,128)} custom-call(s32[64]{0:T(128)} %fusion.starts_ref, f32[8,3072]{1,0:T(8,128)} %concatenate.16.table_ref), custom_call_target="tpu_custom_call" | custom-call | tf_op jit(solution)/shard_map/slots/pallas_call | solution.py:348
  30.4 0.9 convert_element_type.32
  31.3 0.8 reshape.57.local_ref
  34.3 1.6 copy-done.1
  35.8 1.6 copy-done.2
  37.4 14.7 %curvature.1.curve_ref = f32[4096,1]{1,0:T(8,128)S(1)} custom-call(s32[288]{0:T(512)S(1)} %pad_add_fusion.lows_ref, s32[16,1,3072]{2,1,0:T(1,128)S(1)} %copy.39.ids_ref, f32[16,1,3072]{2,1,0:T(1,128)S(1)} %copy.40.nominal_ref, f32[4096,1]{1,0:T(8,128)S(1)} %copy-done.1, f32[4096,1]{1,0:T(8,128)S(1)} %copy-done.2), custom_call_target="tpu_custom_call" | custom-call | tf_op jit(solution)/shard_map/curvature/pallas_call | solution.py:684
  52.1 241.3 %chain.1.templates_ref = bf16[2,4,3,4096,128]{4,3,2,1,0:T(8,128)(2,1)} custom-call(s32[64]{0:T(128)} %fusion.starts_ref, s32[16,1,1216]{2,1,0:T(1,128)} %reshape.57.local_ref, bf16[3072,1536]{1,0:T(8,128)(2,1)} %weights_ref.1, bf16[3072,128]{1,0:T(8,128)(2,1)} %get-tuple-element.16.refs_0_, bf16[3072,128]{1,0:T(8,128)(2,1)} %collective-permute-done.9.refs_1_, ...), custom_call_target="tpu_custom_call" | custom-call | tf_op jit(solution)/shard_map/chain/pallas_call | solution.py:615
  293.5 8.1 %copy-done = bf16[2,4,3,4096,128]{4,3,2,1,0:T(8,128)(2,1)S(1)} copy-done((bf16[2,4,3,4096,128]{4,3,2,1,0:T(8,128)(2,1)S(1)}, bf16[2,4,3,4096,128]{4,3,2,1,0:T(8,128)(2,1)}, u32[]{:S(2)}) %copy-start) | copy-done | bytes 25165848
  301.6 7.7 %weigh.1.weighted_ref = bf16[384,4096]{1,0:T(8,128)(2,1)S(1)} custom-call(s32[1]{0:T(128)} %bitcast.me_ref, f32[4096,1]{1,0:T(8,128)S(1)} %curvature.1.curve_ref, bf16[2,4,3,4096,128]{4,3,2,1,0:T(8,128)(2,1)S(1)} %copy-done), custom_call_target="tpu_custom_call" | custom-call | tf_op jit(solution)/shard_map/weigh/pallas_call | solution.py:723
  309.3 25.2 %hessian.1 = (f32[384,3072]{1,0:T(8,128)}, bf16[384,3072]{1,0:T(8,128)(2,1)S(1)}) custom-call(bf16[384,4096]{1,0:T(8,128)(2,1)S(1)} %weigh.1.weighted_ref, bf16[2,4,3,4096,128]{4,3,2,1,0:T(8,128)(2,1)} %chain.1.templates_ref), custom_call_target="tpu_custom_call" | custom-call | flops 9663676416 | bytes 25165824 | tf_op jit(solution)/shard_map/hessian/pallas_call | solution.py:766
  334.6 2.3 copy-done.3
  336.9 70.5 %sum_over_planes.1 = f32[96,3072]{1,0:T(8,128)S(1)} custom-call(f32[384,3072]{1,0:T(8,128)S(1)} %copy-done.3, bf16[384,3072]{1,0:T(8,128)(2,1)S(1)} %get-tuple-element.12.coded_ref), custom_call_target="tpu_custom_call" | custom-call | tf_op jit(solution)/shard_map/sum_over_planes/pallas_call | solution.py:837
  407.4 1.1 broadcast_multiply_fusion
  (54 shorter events, 7.5 us)
Async XLA Ops:
  0.7 11.5 %collective-permute-start.7 = (f32[2,1024]{1,0:T(2,128)S(1)}, f32[2,1024]{1,0:T(2,128)S(1)}, u32[]{:S(2)}, u32[]{:S(2)}) collective-permute-start(f32[2,1024]{1,0:T(2,128)S(1)} %get-tuple-element.23), channel_id=1, source_target_pairs={{0,4},{2,6},{4,0},{6,2},{8,12},{10,14},{12,8},{14,10},{16,20},{18,... | collective-permute-start | bytes 24584 | tf_op jit(solution)/shard_map/ppermute | solution.py:314
  1.3 11.5 %collective-permute-start.6 = (f32[2,1024]{1,0:T(2,128)S(1)}, f32[2,1024]{1,0:T(2,128)S(1)}, u32[]{:S(2)}, u32[]{:S(2)}) collective-permute-start(f32[2,1024]{1,0:T(2,128)S(1)} %get-tuple-element.23), channel_id=1, source_target_pairs={{0,2},{2,0},{4,6},{6,4},{8,10},{10,8},{12,14},{14,12},{16,18},{18,... | collective-permute-start | bytes 24584 | tf_op jit(solution)/shard_map/ppermute | solution.py:314
  2.8 11.6 %collective-permute-start.8 = (f32[2,1024]{1,0:T(2,128)S(1)}, f32[2,1024]{1,0:T(2,128)S(1)}, u32[]{:S(2)}, u32[]{:S(2)}) collective-permute-start(f32[2,1024]{1,0:T(2,128)S(1)} %get-tuple-element.23), channel_id=1, source_target_pairs={{0,6},{2,4},{4,2},{6,0},{8,14},{10,12},{12,10},{14,8},{16,22},{18,... | collective-permute-start | bytes 24584 | tf_op jit(solution)/shard_map/ppermute | solution.py:314
  5.7 14.5 %collective-permute-start.2 = (f32[2,3072]{1,0:T(2,128)S(1)}, f32[2,3072]{1,0:T(2,128)S(1)}, u32[]{:S(2)}, u32[]{:S(2)}) collective-permute-start(f32[2,3072]{1,0:T(2,128)S(1)} %reshape.54), channel_id=1, source_target_pairs={{0,6},{2,4},{4,2},{6,0},{8,14},{10,12},{12,10},{14,8},{16,22},{18,... | collective-permute-start | bytes 73736 | tf_op jit(solution)/shard_map/ppermute | solution.py:314
  7.2 12.9 %collective-permute-start.1 = (f32[2,3072]{1,0:T(2,128)S(1)}, f32[2,3072]{1,0:T(2,128)S(1)}, u32[]{:S(2)}, u32[]{:S(2)}) collective-permute-start(f32[2,3072]{1,0:T(2,128)S(1)} %reshape.54), channel_id=1, source_target_pairs={{0,4},{2,6},{4,0},{6,2},{8,12},{10,14},{12,8},{14,10},{16,20},{18,... | collective-permute-start | bytes 73736 | tf_op jit(solution)/shard_map/ppermute | solution.py:314
  12.2 8.0 %collective-permute-start = (f32[2,3072]{1,0:T(2,128)S(1)}, f32[2,3072]{1,0:T(2,128)S(1)}, u32[]{:S(2)}, u32[]{:S(2)}) collective-permute-start(f32[2,3072]{1,0:T(2,128)S(1)} %reshape.54), channel_id=1, source_target_pairs={{0,2},{2,0},{4,6},{6,4},{8,10},{10,8},{12,14},{14,12},{16,18},{18,... | collective-permute-start | bytes 73736 | tf_op jit(solution)/shard_map/ppermute | solution.py:314
  12.8 39.3 %collective-permute-start.11 = (bf16[3072,128]{1,0:T(8,128)(2,1)}, bf16[3072,128]{1,0:T(8,128)(2,1)}, u32[]{:S(2)}, u32[]{:S(2)}) collective-permute-start(bf16[3072,128]{1,0:T(8,128)(2,1)} %get-tuple-element.13), channel_id=1, source_target_pairs={{0,6},{2,4},{4,2},{6,0},{8,14},{10,12},{12,10},{14,8},{16,22},{18,... | collective-permute-start | bytes 2359304 | tf_op jit(solution)/shard_map/ppermute | solution.py:314
  14.4 37.8 %collective-permute-start.10 = (bf16[3072,128]{1,0:T(8,128)(2,1)}, bf16[3072,128]{1,0:T(8,128)(2,1)}, u32[]{:S(2)}, u32[]{:S(2)}) collective-permute-start(bf16[3072,128]{1,0:T(8,128)(2,1)} %get-tuple-element.14), channel_id=1, source_target_pairs={{0,4},{2,6},{4,0},{6,2},{8,12},{10,14},{12,8},{14,10},{16,20},{18,... | collective-permute-start | bytes 2359304 | tf_op jit(solution)/shard_map/ppermute | solution.py:314
  20.4 11.8 %collective-permute-start.5 = (f32[4,2,3072]{2,0,1:T(4,128)S(1)}, f32[4,2,3072]{2,0,1:T(4,128)S(1)}, u32[]{:S(2)}, u32[]{:S(2)}) collective-permute-start(f32[4,2,3072]{2,0,1:T(4,128)S(1)} %pad_maximum_fusion), channel_id=1, source_target_pairs={{0,24},{2,26},{4,28},{6,30},{8,0},{10,2},{12,4},{14,6},{16,8},{18,... | collective-permute-start | bytes 294920 | tf_op jit(solution)/shard_map/ppermute | solution.py:314
  20.9 11.8 %collective-permute-start.4 = (f32[4,2,3072]{2,0,1:T(4,128)S(1)}, f32[4,2,3072]{2,0,1:T(4,128)S(1)}, u32[]{:S(2)}, u32[]{:S(2)}) collective-permute-start(f32[4,2,3072]{2,0,1:T(4,128)S(1)} %pad_maximum_fusion), channel_id=1, source_target_pairs={{0,16},{2,18},{4,20},{6,22},{8,24},{10,26},{12,28},{14,30},{16,0},... | collective-permute-start | bytes 294920 | tf_op jit(solution)/shard_map/ppermute | solution.py:314
  21.2 11.5 %collective-permute-start.3 = (f32[4,2,3072]{2,0,1:T(4,128)S(1)}, f32[4,2,3072]{2,0,1:T(4,128)S(1)}, u32[]{:S(2)}, u32[]{:S(2)}) collective-permute-start(f32[4,2,3072]{2,0,1:T(4,128)S(1)} %pad_maximum_fusion), channel_id=1, source_target_pairs={{0,8},{2,10},{4,12},{6,14},{8,16},{10,18},{12,20},{14,22},{16,24},... | collective-permute-start | bytes 294920 | tf_op jit(solution)/shard_map/ppermute | solution.py:314
  32.1 20.0 %collective-permute-start.9 = (bf16[3072,128]{1,0:T(8,128)(2,1)S(1)}, bf16[3072,128]{1,0:T(8,128)(2,1)}, u32[]{:S(2)}, u32[]{:S(2)}) collective-permute-start(bf16[3072,128]{1,0:T(8,128)(2,1)S(1)} %get-tuple-element.15), channel_id=1, source_target_pairs={{0,2},{2,0},{4,6},{6,4},{8,10},{10,8},{12,14},{14,12},{16,18},{18,... | collective-permute-start | bytes 2359304 | tf_op jit(solution)/shard_map/ppermute | solution.py:314
  34.3 1.6 copy-start.1
  35.8 1.6 copy-start.2
  293.5 8.2 %copy-start = (bf16[2,4,3,4096,128]{4,3,2,1,0:T(8,128)(2,1)S(1)}, bf16[2,4,3,4096,128]{4,3,2,1,0:T(8,128)(2,1)}, u32[]{:S(2)}) copy-start(bf16[2,4,3,4096,128]{4,3,2,1,0:T(8,128)(2,1)} %chain.1.templates_ref) | copy-start | bytes 75497472
  334.6 2.3 copy-start.3

commit v3 on v2

--- a/solution.py
+++ b/solution.py
@@ -328,26 +328,23 @@
 
 
 def slots_kernel(bins_dev, starts_ref, table_ref, out_ref):
-    owners, sources, slot = out_ref.shape
+    owners, slot = out_ref.shape
     events = table_ref.shape[1]
     table = table_ref[...]
 
     @pl.loop(0, owners)
     def _(o):
-        for s in range(sources):
-            start = starts_ref[s * owners + o] * 16
-            turned = pltpu.roll(table, lax.rem(events - start, events), axis=1)[s : s + 1, :slot]
-            bins = turned - (o * bins_dev).astype(jnp.float32)
-            inside = (bins >= 0) & (bins < bins_dev)
-            out_ref[o, s : s + 1, :] = jnp.where(inside, bins, -1.0)
-
-
-def slots_of(starts, ids, owners, slot, bins_dev):
-    sources, events = ids.shape
-    table = jnp.concatenate([ids, jnp.zeros((8 - sources, events), jnp.float32)])
+        start = starts_ref[o] * 16
+        turned = pltpu.roll(table, lax.rem(events - start, events), axis=1)[0:1, :slot]
+        bins = turned - (o * bins_dev).astype(jnp.float32)
+        inside = (bins >= 0) & (bins < bins_dev)
+        out_ref[pl.ds(o, 1), :] = jnp.where(inside, bins, -1.0)
+
+
+def slots_of(starts, table, slot, bins_dev):
     return pl.pallas_call(
         functools.partial(slots_kernel, bins_dev),
-        out_shape=jax.ShapeDtypeStruct((owners, sources, slot), jnp.float32),
+        out_shape=jax.ShapeDtypeStruct((starts.shape[0], slot), jnp.float32),
         in_specs=[
             pl.BlockSpec(memory_space=pltpu.SMEM),
             pl.BlockSpec(memory_space=pltpu.VMEM),
@@ -357,15 +354,61 @@
     )(starts, table)
 
 
-def chain_kernel(near, far, chunks, pieces, slot, starts_ref, local_ref, weights_ref, *refs):
+def nominal_kernel(lows_ref, table_ref, out_ref, acc):
+    events = table_ref.shape[1]
+    groups = TILE // LANES
+
+    @pl.loop(0, out_ref.shape[0] // groups)
+    def _(k):
+        bins = (k * TILE + lax.broadcasted_iota(jnp.int32, (TILE, LANES), 0)).astype(jnp.float32)
+
+        def sums(start):
+            part = pl.ds(pl.multiple_of(start, LANES), LANES)
+            return jnp.where(bins == table_ref[0:1, part], table_ref[1:2, part], 0.0)
+
+        first = jnp.minimum(lows_ref[k] // LANES * LANES, events - 2 * LANES)
+        acc[...] = sums(first) + sums(first + LANES)
+        rest = jnp.maximum(lows_ref[k + 1] - first - LANES - 1, 0) // LANES
+
+        @pl.loop(0, rest)
+        def _(e):
+            acc[...] += sums(first + (2 + e) * LANES)
+
+        for h in range(groups):
+            total = jnp.sum(acc[h * LANES : (h + 1) * LANES, :], axis=1, keepdims=True)
+            total = jnp.sum(jnp.where(diagonal(), total, 0.0), axis=0, keepdims=True)
+            out_ref[pl.ds(k * groups + h, 1), :] = total
+
+
+def nominal_sums(lows, table):
+    bins = (lows.shape[0] - 1) * TILE
+    return pl.pallas_call(
+        nominal_kernel,
+        out_shape=jax.ShapeDtypeStruct((bins // LANES, LANES), jnp.float32),
+        in_specs=[
+            pl.BlockSpec(memory_space=pltpu.SMEM),
+            pl.BlockSpec(memory_space=pltpu.VMEM),
+        ],
+        out_specs=pl.BlockSpec(memory_space=pltpu.VMEM),
+        scratch_shapes=[pltpu.VMEM((TILE, LANES), jnp.float32)],
+        name="nominal",
+    )(lows, table)
+
+
+def chain_kernel(
+    near, far, chunks, pieces, slot, starts_ref, local_ref, nominal_ref, data_ref, weights_ref, *refs
+):
     firsts = refs[:near]
-    out_ref = refs[near]
-    rows_refs = refs[near + 1 : near + 1 + chunks]
+    out_ref, curve_ref = refs[near : near + 2]
+    rows_refs = refs[near + 2 : near + 2 + chunks]
     (
+        heads, sums, got_sums, got_side, got_data, levels,
+        head_sem, head_keep, rest_sem, sums_send, sums_recv, total_send, total_recv,
+        data_send, data_recv,
         window, acc, own, send_q, send_s, got_q, got_s,
         row_sem, row_send, row_recv, q_send, q_recv, s_send, s_recv,
         own_sem, side_send, side_recv, pair_send, pair_recv,
-    ) = refs[near + 1 + chunks :]
+    ) = refs[near + 2 + chunks :]
     owners = near * far
     here = lax.axis_index("bins")
     core = lax.axis_index("params")
@@ -374,54 +417,138 @@
     width = chunks * LANES
     held = near // pieces
     size = held * bins_dev
-    lines = size // LANES
+    direct = [d for d in range(1, near) if near != 4 or d != 3]
 
     def side(d):
         return z * near + xor_of(me, d, near)
 
     def along(way):
         return (z + 1 - 2 * way) * near + me
+
+    def peer(k):
+        return lax.rem(z + k, far)
 
     barrier = pltpu.get_barrier_semaphore()
     for d in range(1, near):
         pl.semaphore_signal(barrier, inc=1, device_id={"bins": side(d)}, device_id_type=MESH)
+    for k in range(1, far):
+        pl.semaphore_signal(
+            barrier, inc=1, device_id={"bins": peer(k) * near + me}, device_id_type=MESH
+        )
     pl.semaphore_signal(barrier, inc=1, device_id={"params": 1 - core}, device_id_type=MESH)
-
-    @pl.when(z < far - 1)
-    def _():
-        pl.semaphore_signal(barrier, inc=1, device_id={"bins": along(0)}, device_id_type=MESH)
-
-    @pl.when(z > 0)
-    def _():
-        pl.semaphore_signal(barrier, inc=1, device_id={"bins": along(1)}, device_id_type=MESH)
-
-    inner = (z > 0).astype(jnp.int32) + (z < far - 1).astype(jnp.int32)
-    pl.semaphore_wait(barrier, near + inner)
+    pl.semaphore_wait(barrier, near + far - 1)
+
+    events = weights_ref.shape[0]
+    ahead = firsts[0].shape[0]
+    lower = (z < far // 2).astype(jnp.int32)
+    head_start = lower * (events - ahead)
+    rest_start = (1 - lower) * ahead
 
     def quarter(d, c):
         start = xor_of(me, d, near) * width + c * LANES
-        return weights_ref.at[:, pl.ds(pl.multiple_of(start, LANES), LANES)]
+        return pl.ds(pl.multiple_of(start, LANES), LANES)
+
+    def row_part(c):
+        if c > 0:
+            return pl.ds(0, events)
+        return pl.ds(pl.multiple_of(rest_start, 16), events - ahead)
 
     def row_copy(c, d):
         return pltpu.make_async_remote_copy(
-            src_ref=quarter(d, c),
-            dst_ref=rows_refs[c].at[d],
+            src_ref=weights_ref.at[row_part(c), quarter(d, c)],
+            dst_ref=rows_refs[c].at[d, row_part(c), :],
             send_sem=row_send.at[c, d],
             recv_sem=row_recv.at[c, d],
             device_id={"bins": side(d)},
             device_id_type=MESH,
         )
 
-    def row_local(c, d):
-        source = firsts[d] if c == 0 else quarter(d, c)
-        return pltpu.make_async_copy(source, rows_refs[c].at[d], row_sem.at[c, d])
+    def row_local(c):
+        return pltpu.make_async_copy(
+            weights_ref.at[row_part(c), quarter(0, c)],
+            rows_refs[c].at[0, row_part(c), :],
+            row_sem.at[c],
+        )
+
+    def head_local(d):
+        return pltpu.make_async_copy(firsts[d], heads.at[d], head_sem.at[d])
+
+    def head_stay(d):
+        part = pl.ds(pl.multiple_of(head_start, 16), ahead)
+        return pltpu.make_async_copy(firsts[d], rows_refs[0].at[d, part, :], head_keep.at[d])
+
+    def sums_copy(k):
+        lines_from = pl.ds(pl.multiple_of(peer(k) * curve_ref.shape[0], 8), curve_ref.shape[0])
+        return pltpu.make_async_remote_copy(
+            src_ref=nominal_ref.at[lines_from, :],
+            dst_ref=got_sums.at[k - 1],
+            send_sem=sums_send.at[k - 1],
+            recv_sem=sums_recv.at[k - 1],
+            device_id={"bins": peer(k) * near + me},
+            device_id_type=MESH,
+        )
+
+    def total_copy(d):
+        return pltpu.make_async_remote_copy(
+            src_ref=sums,
+            dst_ref=got_side.at[d - 1],
+            send_sem=total_send.at[d - 1],
+            recv_sem=total_recv.at[d - 1],
+            device_id={"bins": side(d)},
+            device_id_type=MESH,
+        )
+
+    def data_copy(d):
+        return pltpu.make_async_remote_copy(
+            src_ref=data_ref,
+            dst_ref=got_data.at[d - 1],
+            send_sem=data_send.at[d - 1],
+            recv_sem=data_recv.at[d - 1],
+            device_id={"bins": side(d)},
+            device_id_type=MESH,
+        )
 
     for d in range(near):
-        row_local(0, d).start()
-    for c in range(1, chunks):
-        row_local(c, 0).start()
+        head_local(d).start()
+    for k in range(1, far):
+        sums_copy(k).start()
+    for d in range(1, near):
+        data_copy(d).start()
+    for c in range(chunks):
         for d in range(1, near):
             row_copy(c, d).start()
+    for c in range(chunks):
+        row_local(c).start()
+    for d in range(near):
+        head_stay(d).start()
+
+    def gather_sums():
+        own_lines = pl.ds(pl.multiple_of(z * curve_ref.shape[0], 8), curve_ref.shape[0])
+        total = nominal_ref[own_lines, :]
+        for k in range(1, far):
+            sums_copy(k).wait_recv()
+            total += got_sums[k - 1]
+        sums[...] = total
+        for d in range(1, near):
+            total_copy(d).start()
+
+    def finish_sums():
+        total = sums[...]
+        for d in range(1, near):
+            total_copy(d).wait_recv()
+            total += got_side[d - 1]
+        lines_dev = bins_dev // LANES
+        levels[0, pl.ds(pl.multiple_of(me * lines_dev, 8), lines_dev), :] = data_ref[0:lines_dev, :]
+        levels[1, pl.ds(pl.multiple_of(me * lines_dev, 8), lines_dev), :] = data_ref[
+            lines_dev : 2 * lines_dev, :
+        ]
+        for d in range(1, near):
+            data_copy(d).wait_recv()
+            part = pl.ds(pl.multiple_of(xor_of(me, d, near) * lines_dev, 8), lines_dev)
+            levels[0, part, :] = got_data[d - 1, 0:lines_dev, :]
+            levels[1, part, :] = got_data[d - 1, lines_dev : 2 * lines_dev, :]
+        yields = levels[0] + total
+        curve_ref[...] = levels[1] / (yields * yields)
 
     def chain_copies(way, c, r, p):
         return [
@@ -438,13 +565,18 @@
             )
         ]
 
-    def fold(c, plane, p, inputs, finish):
+    def fold(c, plane, p, inputs, finish, early=False):
         @pl.loop(0, held)
         def _(i):
             owner = plane * near + p * held + i
             for s in range(near):
-                start = starts_ref[s * owners + owner] * 16
-                window[s * slot : (s + 1) * slot, :] = rows_refs[c][s, pl.ds(start, slot), :]
+                start = starts_ref[s * owners + owner]
+                if early:
+                    start = jnp.maximum(start - lower * ((events - ahead) // 16), 0)
+                    part = heads[s, pl.ds(start * 16, slot), :]
+                else:
+                    part = rows_refs[c][s, pl.ds(start * 16, slot), :]
+                window[s * slot : (s + 1) * slot, :] = part
 
             @pl.loop(0, bins_dev // TILE)
             def _(k):
@@ -486,9 +618,10 @@
                     def _():
                         has = step_in > 0
 
-                        @pl.when(has)
-                        def _():
-                            wait_chain(way, c, r - 1, p)
+                        if first > 1:
+                            @pl.when(has)
+                            def _():
+                                wait_chain(way, c, r - 1, p)
 
                         def code(value, line, part, eye):
                             most = jnp.max(jnp.abs(value), axis=1, keepdims=True)
@@ -502,20 +635,23 @@
                             )
 
                         plane = z + (far - r) * (1 - 2 * way)
-                        fold(c, plane, p, [(way, r - 1, has)], code)
+                        early = c == 0 and first == 1
+                        fold(c, plane, p, [] if first == 1 else [(way, r - 1, has)], code, early)
                         for copy in chain_copies(way, c, r, p):
                             copy.start()
 
     def rows_part(p):
         return pl.ds(pl.multiple_of(p * size, size), size)
 
-    def side_copy(c, d, p):
+    def side_copy(c, d, p, source=0, hop=None):
+        hop = d if hop is None else hop
+        origin = own.at[c] if source == 0 else out_ref.at[0, source, c]
         return pltpu.make_async_remote_copy(
-            src_ref=own.at[c, rows_part(p), :],
+            src_ref=origin.at[rows_part(p), :],
             dst_ref=out_ref.at[0, d, c, rows_part(p), :],
             send_sem=side_send.at[c, d, p],
             recv_sem=side_recv.at[c, d, p],
-            device_id={"bins": side(d)},
+            device_id={"bins": side(hop)},
             device_id_type=MESH,
         )
 
@@ -551,45 +687,86 @@
                 own[c, row, :] = value.astype(own.dtype)
 
             fold(c, z, p, [(0, far - 1, z > 0), (1, far - 1, z < far - 1)], store)
-            for d in range(1, near):
+            for d in direct:
                 side_copy(c, d, p).start()
             pair_copy(c, 0, p).start()
             keep_copy(c, p).start()
 
+    def forward(c, p, act):
+        if near == 4:
+            @pl.when(lax.rem(p, 2) == 0)
+            def _():
+                act(side_copy(c, 3, p, 1, 2))
+
+            @pl.when(lax.rem(p, 2) == 1)
+            def _():
+                act(side_copy(c, 3, p, 2, 1))
+
     def relay(c):
         @pl.loop(0, pieces)
         def _(p):
+            for d in direct:
+                side_copy(c, d, p).wait_recv()
+            forward(c, p, lambda copy: copy.start())
+            for d in direct:
+                pair_copy(c, d, p).start()
+
+    def relay_last(c):
+        @pl.loop(0, pieces)
+        def _(p):
             for d in range(1, near):
-                side_copy(c, d, p).wait_recv()
-                pair_copy(c, d, p).start()
-
+                if d not in direct:
+                    side_copy(c, d, p).wait_recv()
+                    pair_copy(c, d, p).start()
+
+    for d in range(near):
+        head_local(d).wait()
     for c in range(chunks):
-        row_local(c, 0).wait()
-        for d in range(1, near):
-            if c == 0:
-                row_local(c, d).wait()
-            else:
+        if c > 0:
+            row_local(c).wait()
+            for d in range(1, near):
                 row_copy(c, d).wait_recv()
         rounds(c, 1, 2)
+        if c == 0:
+            row_local(c).wait()
+            head_stay(0).wait()
+            for d in range(1, near):
+                head_stay(d).wait()
+                row_copy(c, d).wait_recv()
         if c > 0:
             finish(c - 1)
         rounds(c, 2, far)
-        if 0 < c < chunks - 1:
+        if c == 0:
+            gather_sums()
+        if c == 1:
+            finish_sums()
+        if c > 0:
             relay(c - 1)
+        if c > 1:
+            relay_last(c - 2)
+    if chunks == 1:
+        finish_sums()
     finish(chunks - 1)
-    for c in range(max(chunks - 2, 0), chunks):
-        relay(c)
-
+    if chunks > 1:
+        relay_last(chunks - 2)
+    relay(chunks - 1)
+    relay_last(chunks - 1)
+
+    for k in range(1, far):
+        sums_copy(k).wait_send()
+    for d in range(1, near):
+        total_copy(d).wait_send()
+        data_copy(d).wait_send()
     for c in range(chunks):
-        if c > 0:
-            for d in range(1, near):
-                row_copy(c, d).wait_send()
+        for d in range(1, near):
+            row_copy(c, d).wait_send()
 
         @pl.loop(0, pieces)
         def _(p):
             keep_copy(c, p).wait()
-            for d in range(1, near):
+            for d in direct:
                 side_copy(c, d, p).wait_send()
+            forward(c, p, lambda copy: copy.wait_send())
             for d in range(near):
                 pair_copy(c, d, p).wait_send()
                 pair_copy(c, d, p).wait_recv()
@@ -605,32 +782,55 @@
                             copy.wait_send()
 
 
-def chain(starts, local, weights, firsts, near, far, chunks, slot, bins_dev):
+def chain(starts, local, nominal, data, weights, firsts, near, far, chunks, slot, bins_dev):
     events = weights.shape[0]
-    pieces = 2
+    ahead = firsts[0].shape[0]
+    pieces = near
     bins = near * bins_dev
     size = bins // pieces
     hops = (2, chunks, far - 1, pieces)
+    lines = bins // LANES
     dma = pltpu.SemaphoreType.DMA
+    rows = jnp.bfloat16
+    table = jnp.float32
     return pl.pallas_call(
         functools.partial(chain_kernel, near, far, chunks, pieces, slot),
-        out_shape=jax.ShapeDtypeStruct((2, near, chunks, bins, LANES), jnp.bfloat16),
-        in_specs=[
-            pl.BlockSpec(memory_space=pltpu.SMEM),
+        out_shape=[
+            jax.ShapeDtypeStruct((2, near, chunks, bins, LANES), rows),
+            jax.ShapeDtypeStruct((lines, LANES), table),
+        ],
+        in_specs=[pl.BlockSpec(memory_space=pltpu.SMEM)]
+        + [pl.BlockSpec(memory_space=pltpu.VMEM)] * 3
+        + [pl.BlockSpec(memory_space=pl.ANY)] * (1 + near),
+        out_specs=[
+            pl.BlockSpec(memory_space=pl.ANY),
             pl.BlockSpec(memory_space=pltpu.VMEM),
-        ]
-        + [pl.BlockSpec(memory_space=pl.ANY)] * (1 + near),
-        out_specs=pl.BlockSpec(memory_space=pl.ANY),
-        scratch_shapes=[pltpu.VMEM((near, events, LANES), jnp.bfloat16)] * chunks
+        ],
+        scratch_shapes=[pltpu.VMEM((near, events, LANES), rows)] * chunks
         + [
-            pltpu.VMEM((near * slot, LANES), jnp.bfloat16),
-            pltpu.VMEM((TILE, LANES), jnp.float32),
-            pltpu.VMEM((chunks, bins, LANES), jnp.bfloat16),
+            pltpu.VMEM((near, ahead, LANES), rows),
+            pltpu.VMEM((lines, LANES), table),
+            pltpu.VMEM((far - 1, lines, LANES), table),
+            pltpu.VMEM((near - 1, lines, LANES), table),
+            pltpu.VMEM((near - 1,) + data.shape, table),
+            pltpu.VMEM((2, lines, LANES), table),
+            dma((near,)),
+            dma((near,)),
+            dma((1,)),
+            dma((far - 1,)),
+            dma((far - 1,)),
+            dma((near - 1,)),
+            dma((near - 1,)),
+            dma((near - 1,)),
+            dma((near - 1,)),
+            pltpu.VMEM((near * slot, LANES), rows),
+            pltpu.VMEM((TILE, LANES), table),
+            pltpu.VMEM((chunks, bins, LANES), rows),
             pltpu.VMEM(hops + (size, LANES), jnp.int16),
-            pltpu.VMEM(hops + (size // LANES, LANES), jnp.float32),
+            pltpu.VMEM(hops + (size // LANES, LANES), table),
             pltpu.VMEM(hops + (size, LANES), jnp.int16),
-            pltpu.VMEM(hops + (size // LANES, LANES), jnp.float32),
-            dma((chunks, near)),
+            pltpu.VMEM(hops + (size // LANES, LANES), table),
+            dma((chunks,)),
             dma((chunks, near)),
             dma((chunks, near)),
             dma(hops),
@@ -644,151 +844,23 @@
             dma((chunks, near, pieces)),
         ],
         compiler_params=pltpu.CompilerParams(
-            collective_id=3, has_side_effects=True, vmem_limit_bytes=60 << 20
+            collective_id=3, has_side_effects=True, vmem_limit_bytes=62 << 20
         ),
         name="chain",
-    )(starts, local, weights, *firsts)
-
-
-def curve_kernel(lows_ref, ids_ref, nominal_ref, background_ref, observed_ref, out_ref, acc):
-    sources = ids_ref.shape[0]
-    bounds = lows_ref.shape[0] // sources
-    index = pl.program_id(0)
-    first_bin = lows_ref[sources * (bounds - 1)]
-    bins = first_bin + index * TILE + lax.broadcasted_iota(jnp.int32, (TILE, LANES), 0)
-    acc[...] = jnp.zeros_like(acc)
-
-    @pl.loop(0, sources)
-    def _(s):
-        low = lows_ref[s * (bounds - 1) + index]
-        high = lows_ref[s * (bounds - 1) + index + 1]
-
-        @pl.loop(low // LANES, (high + LANES - 1) // LANES)
-        def _(b):
-            part = pl.ds(pl.multiple_of(b * LANES, LANES), LANES)
-            hit = bins == ids_ref[s, :, part]
-            acc[...] += jnp.where(hit, nominal_ref[s, :, part], 0.0)
-
-    yields = background_ref[...] + jnp.sum(acc[...], axis=1, keepdims=True)
-    out_ref[...] = observed_ref[...] / (yields * yields)
-
-
-def curvature_of(lows, first_bin, ids, nominal, background, observed):
-    sources, events = ids.shape
-    bins = background.shape[0]
-    table = jnp.concatenate(
-        [lows.reshape(-1), first_bin.reshape(1), jnp.zeros((sources - 1,), jnp.int32)]
-    )
-    column = pl.BlockSpec((TILE, 1), lambda j: (j, 0))
-    whole = pl.BlockSpec((sources, 1, events), lambda j: (0, 0, 0))
-    return pl.pallas_call(
-        curve_kernel,
-        grid=(bins // TILE,),
-        out_shape=jax.ShapeDtypeStruct((bins, 1), jnp.float32),
-        in_specs=[pl.BlockSpec(memory_space=pltpu.SMEM), whole, whole, column, column],
-        out_specs=column,
-        scratch_shapes=[pltpu.VMEM((TILE, LANES), jnp.float32)],
-        compiler_params=pltpu.CompilerParams(
-            vmem_limit_bytes=8 << 20, dimension_semantics=("arbitrary",)
-        ),
-        name="curvature",
-    )(
-        table,
-        ids.reshape(sources, 1, events),
-        nominal.reshape(sources, 1, events),
-        background.reshape(bins, 1),
-        observed.reshape(bins, 1),
-    )
-
-
-def weigh_kernel(piece, me_ref, curve_ref, templates_ref, out_ref):
-    _, near, chunks, _, _ = templates_ref.shape
-    rows = lax.broadcasted_iota(jnp.int32, (piece, LANES), 0) + me_ref[0] * piece
-    lanes = lax.broadcasted_iota(jnp.int32, (piece, LANES), 1)
-    for d in range(near):
-        total = 0.0
-        for c in range(chunks):
-            pick = (rows == lanes + c * LANES).astype(jnp.bfloat16)
-            value = curve_ref[...] * templates_ref[0, d, c].astype(jnp.float32)
-            total += lax.dot_general(
-                pick, value.astype(jnp.bfloat16), (((1,), (1,)), ((), ())),
-                preferred_element_type=jnp.float32,
-            )
-        out_ref[d * piece : (d + 1) * piece, :] = total.astype(out_ref.dtype)
-
-
-def weigh(me, curve, templates, piece):
-    _, near, chunks, bins, _ = templates.shape
-    tile = 512
-    return pl.pallas_call(
-        functools.partial(weigh_kernel, piece),
-        grid=(bins // tile,),
-        out_shape=jax.ShapeDtypeStruct((near * piece, bins), jnp.bfloat16),
-        in_specs=[
-            pl.BlockSpec(memory_space=pltpu.SMEM),
-            pl.BlockSpec((tile, 1), lambda j: (j, 0)),
-            pl.BlockSpec((1, near, chunks, tile, LANES), lambda j: (0, 0, 0, j, 0)),
-        ],
-        out_specs=pl.BlockSpec((near * piece, tile), lambda j: (0, j)),
-        compiler_params=pltpu.CompilerParams(
-            vmem_limit_bytes=24 << 20, dimension_semantics=("arbitrary",)
-        ),
-        name="weigh",
-    )(me, curve, templates)
-
-
-def hessian_kernel(weighted_ref, templates_ref, full_ref, coded_ref, held, sems):
-    groups, near, chunks, _, _ = templates_ref.shape
-    places = [(k, d, c) for k in range(groups) for d in range(near) for c in range(chunks)]
-
-    def fetch(n):
-        return pltpu.make_async_copy(
-            templates_ref.at[places[n]], held.at[:, n * LANES : (n + 1) * LANES], sems.at[n]
-        )
-
-    for n in range(len(places)):
-        fetch(n).start()
-    for n in range(0, len(places), 2):
-        fetch(n).wait()
-        fetch(n + 1).wait()
-        columns = slice(n * LANES, (n + 2) * LANES)
-        total = jnp.dot(
-            weighted_ref[...], held[:, columns], preferred_element_type=jnp.float32
-        )
-        full_ref[:, columns] = total
-        coded_ref[:, columns] = total.astype(coded_ref.dtype)
-
-
-def hessian_of(weighted, templates):
-    rows, bins = weighted.shape
-    count = math.prod(templates.shape[:3])
-    shape = (rows, count * LANES)
-    return pl.pallas_call(
-        hessian_kernel,
-        out_shape=[
-            jax.ShapeDtypeStruct(shape, jnp.float32),
-            jax.ShapeDtypeStruct(shape, jnp.bfloat16),
-        ],
-        in_specs=[pl.BlockSpec(memory_space=pltpu.VMEM), pl.BlockSpec(memory_space=pl.ANY)],
-        out_specs=[pl.BlockSpec(memory_space=pltpu.VMEM)] * 2,
-        scratch_shapes=[
-            pltpu.VMEM((bins, count * LANES), jnp.bfloat16),
-            pltpu.SemaphoreType.DMA((count,)),
-        ],
-        compiler_params=pltpu.CompilerParams(vmem_limit_bytes=48 << 20),
-        cost_estimate=pl.CostEstimate(
-            flops=2 * rows * bins * count * LANES,
-            bytes_accessed=2 * bins * count * LANES,
-            transcendentals=0,
-        ),
-        name="hessian",
-    )(weighted, templates)
-
-
-def sum_kernel(near, far, piece, run, full_ref, coded_ref, out_ref, own, got, own_sem, sends, recvs):
+    )(starts, local, nominal, data, weights, *firsts)
+
+
+def tail_kernel(
+    near, far, templates_ref, curve_ref, out_ref, held, weighted, total, coded, own, got,
+    sems, sends, recvs,
+):
+    groups, _, chunks, bins, _ = templates_ref.shape
     here = lax.axis_index("bins")
     z, me = here // near, lax.rem(here, near)
-    columns = out_ref.shape[1]
+    piece = own.shape[0]
+    count = groups * near * chunks
+    step = 2 * LANES
+    depth = 4 * LANES
 
     def peer(k):
         return lax.rem(z + k, far)
@@ -798,59 +870,124 @@
         pl.semaphore_signal(
             barrier, inc=1, device_id={"bins": peer(k) * near + me}, device_id_type=MESH
         )
+
+    def fetch(n):
+        part = templates_ref.at[n // (near * chunks), lax.rem(n // chunks, near), lax.rem(n, chunks)]
+        return pltpu.make_async_copy(
+            part, held.at[:, pl.ds(pl.multiple_of(n * LANES, LANES), LANES)], sems.at[n]
+        )
+
+    @pl.loop(0, count)
+    def _(n):
+        fetch(n).start()
+
     pl.semaphore_wait(barrier, far - 1)
+    rows = lax.broadcasted_iota(jnp.int32, (piece, LANES), 0) + me * piece
+    lanes = lax.broadcasted_iota(jnp.int32, (piece, LANES), 1)
+
+    @pl.loop(0, near * chunks)
+    def _(n):
+        fetch(n).wait()
+
+    @pl.loop(0, bins // depth)
+    def _(b):
+        eye = diagonal()
+        curves = []
+        for h in range(depth // LANES):
+            line = curve_ref[pl.ds(b * (depth // LANES) + h, 1), :]
+            curves.append(jnp.sum(jnp.where(eye, line, 0.0), axis=1, keepdims=True))
+        curve = jnp.concatenate(curves, axis=0)
+        part = pl.ds(pl.multiple_of(b * depth, depth), depth)
+        for d in range(near):
+            picked = 0.0
+            for c in range(chunks):
+                pick = (rows == lanes + c * LANES).astype(jnp.bfloat16)
+                columns = slice((d * chunks + c) * LANES, (d * chunks + c + 1) * LANES)
+                value = curve * held[part, columns].astype(jnp.float32)
+                picked += lax.dot_general(
+                    pick, value.astype(jnp.bfloat16), (((1,), (1,)), ((), ())),
+                    preferred_element_type=jnp.float32,
+                )
+            weighted[d * piece : (d + 1) * piece, part] = picked.astype(weighted.dtype)
 
     def rows_for(target):
-        return pl.ds(pl.multiple_of(xor_of(me, target, near) * piece, piece), piece)
-
-    def copy(k):
+        return pl.ds(pl.multiple_of(xor_of(me, target, near) * piece, 16), piece)
+
+    def columns_of(n):
+        return pl.ds(pl.multiple_of(n * step, step), step)
+
+    def copy(k, n):
         return pltpu.make_async_remote_copy(
-            src_ref=coded_ref.at[rows_for(peer(k)), :],
-            dst_ref=got.at[k - 1],
-            send_sem=sends.at[k - 1],
-            recv_sem=recvs.at[k - 1],
+            src_ref=coded.at[rows_for(peer(k)), columns_of(n)],
+            dst_ref=got.at[k - 1, :, columns_of(n)],
+            send_sem=sends.at[k - 1, n],
+            recv_sem=recvs.at[k - 1, n],
             device_id={"bins": peer(k) * near + me},
             device_id_type=MESH,
         )
 
-    for k in range(1, far):
-        copy(k).start()
-    own_copy = pltpu.make_async_copy(full_ref.at[rows_for(z), :], own, own_sem)
-    own_copy.start()
-    own_copy.wait()
-    for k in range(1, far):
-        copy(k).wait_recv()
-    for n in range(columns // run):
-        group, d = n // near, n % near
-        total = own[:, n * run : (n + 1) * run]
+    @pl.loop(0, count // 2)
+    def _(n):
+        @pl.when(n >= near * chunks // 2)
+        def _():
+            fetch(2 * n).wait()
+            fetch(2 * n + 1).wait()
+
+        total[...] = jnp.dot(
+            weighted[...], held[:, columns_of(n)], preferred_element_type=jnp.float32
+        )
+        coded[:, columns_of(n)] = total[...].astype(coded.dtype)
+        own[:, columns_of(n)] = total[rows_for(z), :]
         for k in range(1, far):
-            total += got[k - 1, :, n * run : (n + 1) * run].astype(jnp.float32)
-        start = (group * near + xor_of(me, d, near)) * run
-        out_ref[:, pl.ds(pl.multiple_of(start, LANES), run)] = total
-    for k in range(1, far):
-        copy(k).wait_send()
-
-
-def sum_over_planes(full, coded, near, far, run):
-    rows, columns = full.shape
-    piece = rows // far
+            copy(k, n).start()
+
+    @pl.loop(0, count // 2)
+    def _(n):
+        for k in range(1, far):
+            copy(k, n).wait_recv()
+        for half in range(2):
+            place = 2 * n + half
+            group = place // (near * chunks)
+            d = lax.rem(place // chunks, near)
+            start = ((group * near + xor_of(me, d, near)) * chunks + lax.rem(place, chunks)) * LANES
+            part = pl.ds(pl.multiple_of(place * LANES, LANES), LANES)
+            value = own[:, part]
+            for k in range(1, far):
+                value += got[k - 1, :, part].astype(jnp.float32)
+            out_ref[:, pl.ds(pl.multiple_of(start, LANES), LANES)] = value
+
+    @pl.loop(0, count // 2)
+    def _(n):
+        for k in range(1, far):
+            copy(k, n).wait_send()
+
+
+def tail(templates, curve, near, far):
+    groups, _, chunks, bins, _ = templates.shape
+    piece = chunks * LANES // far
+    columns = groups * near * chunks * LANES
+    count = groups * near * chunks
     return pl.pallas_call(
-        functools.partial(sum_kernel, near, far, piece, run),
+        functools.partial(tail_kernel, near, far),
         out_shape=jax.ShapeDtypeStruct((piece, columns), jnp.float32),
-        in_specs=[pl.BlockSpec(memory_space=pl.ANY)] * 2,
+        in_specs=[pl.BlockSpec(memory_space=pl.ANY), pl.BlockSpec(memory_space=pltpu.VMEM)],
         out_specs=pl.BlockSpec(memory_space=pltpu.VMEM),
         scratch_shapes=[
+            pltpu.VMEM((bins, columns), jnp.bfloat16),
+            pltpu.VMEM((near * piece, bins), jnp.bfloat16),
+            pltpu.VMEM((near * piece, 2 * LANES), jnp.float32),
+            pltpu.VMEM((near * piece, columns), jnp.bfloat16),
             pltpu.VMEM((piece, columns), jnp.float32),
-            pltpu.VMEM((far - 1, piece, columns), coded.dtype),
-            pltpu.SemaphoreType.DMA,
-            pltpu.SemaphoreType.DMA((far - 1,)),
-            pltpu.SemaphoreType.DMA((far - 1,)),
+            pltpu.VMEM((far - 1, piece, columns), jnp.bfloat16),
+            pltpu.SemaphoreType.DMA((count,)),
+            pltpu.SemaphoreType.DMA((far - 1, count // 2)),
+            pltpu.SemaphoreType.DMA((far - 1, count // 2)),
         ],
         compiler_params=pltpu.CompilerParams(
-            collective_id=2, has_side_effects=True, vmem_limit_bytes=16 << 20
+            collective_id=2, has_side_effects=True, vmem_limit_bytes=60 << 20
         ),
-        name="sum_over_planes",
-    )(full, coded)
+        name="tail",
+    )(templates, curve)
 
 
 def body_by_parameters(event_bins, event_weights, nominal, background, observed):
@@ -861,9 +998,9 @@
     bins_dev = background.shape[0]
     width = event_weights.shape[1] // near
     chunks = width // LANES
-    bins = near * bins_dev
     capacity = 3 * events // (2 * owners)
     slot = -(-capacity // 16) * 16 + 16
+    ahead = min(-(-near * capacity // 16) * 16 + 16, events - 16)
     here = lax.axis_index("bins")
     z, me = here // near, lax.rem(here, near)
     around = [[(s, s // near * near + (s % near ^ d)) for s in range(owners)] for d in range(near)]
@@ -871,41 +1008,31 @@
     def spread(value):
         return [value] + [shift(value, around[d]) for d in range(1, near)]
 
-    meta = jnp.concatenate([event_bins.astype(jnp.float32), nominal.astype(jnp.float32)])
-    meta = jnp.stack(spread(meta.reshape(2, events)))
-    local = jnp.stack(spread(jnp.stack([background, observed])))
-    ids = meta[:, 0]
-    marks = (jnp.arange(owners, dtype=jnp.int32) * bins_dev).astype(jnp.float32)
-    before = jnp.sum((ids[:, None, :] < marks[None, :, None]).astype(jnp.int32), axis=2)
-    starts = jnp.minimum(before // 16, (events - slot) // 16).reshape(-1)
-    places = slots_of(starts, ids, owners, slot, bins_dev)
-    places = places.astype(jnp.int32).reshape(owners, 1, near * slot)
+    marks = jnp.arange(owners * bins_dev // TILE + 1, dtype=jnp.int32) * TILE
+    lows = jnp.sum((event_bins[None, :] < marks[:, None]).astype(jnp.int32), axis=1)
+    starts = jnp.minimum(lows[: -1 : bins_dev // TILE] // 16, (events - slot) // 16)
+    table = jnp.stack([event_bins.astype(jnp.float32), nominal.astype(jnp.float32)])
+    table = jnp.concatenate([table, jnp.zeros((6, events), jnp.float32)])
+    places = slots_of(starts, table, slot, bins_dev)
+    line = jnp.pad(starts.astype(jnp.float32), (0, slot - owners)).reshape(1, slot)
+    places = jnp.stack(spread(jnp.concatenate([places, line])))
 
     firsts = []
+    first_row = jnp.where(z < far // 2, events - ahead, 0)
     for d in range(near):
-        part = lax.dynamic_slice(event_weights, (0, (me ^ d) * width), (events, LANES))
+        corner = (first_row, (me ^ d) * width)
+        part = lax.dynamic_slice(event_weights, corner, (ahead, LANES))
         firsts.append(part if d == 0 else shift(part, around[d]))
 
-    metas = [meta] + [
-        shift(meta, [(s, (s + k * near) % owners) for s in range(owners)]) for k in range(1, far)
-    ]
-    metas = jnp.concatenate(metas)
-    all_ids = metas[:, 0].astype(jnp.int32)
-    first_bin = z * bins
-    near_marks = first_bin + jnp.arange(bins // TILE + 1, dtype=jnp.int32) * TILE
-    lows = jnp.sum((all_ids[:, None, :] < near_marks[None, :, None]).astype(jnp.int32), axis=2)
-    index = jnp.arange(near, dtype=jnp.int32)
-    match = (index[None, :] ^ me) == index[:, None]
-    local = jnp.sum(jnp.where(match[:, :, None, None], local[None], 0.0), axis=1)
-    curve = curvature_of(
-        lows, first_bin, all_ids, metas[:, 1], local[:, 0].reshape(-1), local[:, 1].reshape(-1)
+    sums = nominal_sums(lows, table)
+    starts = places[:, owners, :owners].astype(jnp.int32).reshape(-1)
+    places = places[:, :owners].astype(jnp.int32).transpose(1, 0, 2)
+    places = places.reshape(owners, 1, near * slot)
+    data = jnp.concatenate([background, observed]).reshape(-1, LANES)
+    templates, curve = chain(
+        starts, places, sums, data, event_weights, firsts, near, far, chunks, slot, bins_dev
     )
-
-    starts, curve = lax.optimization_barrier((starts, curve))
-    templates = chain(starts, places, event_weights, firsts, near, far, chunks, slot, bins_dev)
-    weighted = weigh(me.reshape(1).astype(jnp.int32), curve, templates, width // far)
-    full, coded = hessian_of(weighted, templates)
-    summed = sum_over_planes(full, coded, near, far, width)
+    summed = tail(templates, curve, near, far)
     return summed * (1.0 / (bins_dev * owners))
 
 

time: 411 us -> 354 us (0.86)
  Pallas kernels: 364 us -> 328 us
  local copies, waits for them, and re-layouts: 23.6 us -> 4.75 us
  starting transfers between devices: 14.7 us -> 6.92 us
  waiting for transfers between devices: 0.03 us -> 5.62 us
    pallas_call x1, Pallas kernels: 241 us -> 222 us  [chain(): pl.pallas_call(functools.partial(chain_kernel, near, far, chunks, pieces,...]
    pallas_call x4 -> x2, Pallas kernels: 118 us -> 102 us  [the longest x1 90.8 us: tail(): pl.pallas_call(functools.partial(tail_kernel, near, far), out_shape=jax.S...]
    unnamed x8 -> x16, local copies, waits for them, and re-layouts: 13.7 us -> 0.94 us
    ppermute x12 -> x6, starting transfers between devices: 14.7 us -> 6.92 us  [shift(): return lax.ppermute(value, 'bins', pairs)]
    ppermute x12 -> x6, waiting for transfers between devices: 0.03 us -> 5.62 us  [shift(): return lax.ppermute(value, 'bins', pairs)]
  transfers between devices with their start and end apart: 12 -> 6, of which waited for: 0 -> 1; matrix products, arithmetic and copies ran while one was open for 3% -> 1% of each run, Pallas kernels for 5% -> 4%
where the time goes in v3:
time: 354 us; the launch traced here: 350 us
  Pallas kernels  328 us (93%)
  starting transfers between devices  6.92 us (2%)
  waiting for transfers between devices  5.62 us (2%)
  other arithmetic  5.27 us (1%)
  local copies, waits for them, and re-layouts  4.75 us (1%)
    pallas_call x1, Pallas kernels, chain(): pl.pallas_call(functools.partial(chain_kernel, near, far, chunks, pieces,...  222 us
    pallas_call x1, Pallas kernels, tail(): pl.pallas_call(functools.partial(tail_kernel, near, far), out_shape=jax.S...  90.8 us
    pallas_call x1, Pallas kernels, nominal_sums(): pl.pallas_call(nominal_kernel, out_shape=jax.ShapeDtypeStruct((bins // LA...  11.4 us
  transfers between devices with their start and end apart: 6, of which 1 were waited for; matrix products, arithmetic and copies ran while one was open for 1% of the time, Pallas kernels for 4%

profile of v3, /device:TPU:28, one launch (start us, length us, event | category | flops | bytes accessed | tf_op | source)
XLA Modules:
  0.0 350.5 jit_solution(13950825022242679341)
XLA Ops:
  0.0 2.1 fusion.7
  2.1 1.4 collective-permute-start.5
  3.6 1.5 collective-permute-start.4
  5.1 0.5 collective-permute-start.3
  5.6 0.3 convert_reduce_fusion.lows_ref
  5.9 0.1 slice.9
  6.0 0.5 fusion.5
  6.6 0.1 pad.15.clone
  6.6 0.7 maximum_maximum_fusion.table_ref
  7.3 3.4 slots.1
  10.7 0.7 fusion.4
  11.4 0.5 collective-permute-start.1
  12.0 1.5 collective-permute-start
  13.4 5.6 %collective-permute-done.1 = f32[17,304]{1,0:T(8,128)S(1)} collective-permute-done((f32[17,304]{1,0:T(8,128)S(1)}, f32[17,304]{1,0:T(8,128)S(1)}, u32[]{:S(2)}, u32[]{:S(2)}) %collective-permute-start.1) | collective-permute-done | bytes 20704 | tf_op jit(solution)/shard_map/ppermute | solution.py:314
  19.0 1.4 collective-permute-start.2
  20.5 0.6 pad_maximum_fusion.4.data_ref
  21.1 11.4 %nominal.1.nominal_ref = f32[128,128]{1,0:T(8,128)} custom-call(s32[65]{0:T(128)} %copy-done.7, f32[8,3072]{1,0:T(8,128)} %maximum_maximum_fusion.table_ref), custom_call_target="tpu_custom_call" | custom-call | tf_op jit(solution)/shard_map/nominal/pallas_call | solution.py:385
  32.5 0.7 convert_element_type.26.starts_ref
  33.2 0.8 reshape.18.local_ref
  34.1 0.7 copy-done
  34.8 0.2 copy-done.1
  35.0 222.3 %chain.1 = (bf16[2,4,3,4096,128]{4,3,2,1,0:T(8,128)(2,1)}, f32[32,128]{1,0:T(8,128)}) custom-call(s32[64]{0:T(128)} %convert_element_type.26.starts_ref, s32[16,1,1216]{2,1,0:T(1,128)} %reshape.18.local_ref, f32[128,128]{1,0:T(8,128)} %nominal.1.nominal_ref, f32[16,128]{1,0:T(8,128)} %pad_maximum_fusion.4.data_ref, bf16[3072,1536]{1,0:T(8,128)(2,1)} %weights_ref.1, ...), custom_call_target="tpu_custom_call" | custom-call | tf_op jit(solution)/shard_map/chain/pallas_call | solution.py:796
  257.3 90.8 %tail.1 = f32[96,3072]{1,0:T(8,128)} custom-call(bf16[2,4,3,4096,128]{4,3,2,1,0:T(8,128)(2,1)} %get-tuple-element.7.templates_ref, f32[32,128]{1,0:T(8,128)} %get-tuple-element.8.curve_ref), custom_call_target="tpu_custom_call" | custom-call | tf_op jit(solution)/shard_map/tail/pallas_call | solution.py:970
  348.1 2.4 broadcast_multiply_fusion
  (28 shorter events, 0.2 us)
Async XLA Ops:
  0.0 5.6 %copy-start.3 = (s32[3072]{0:T(1024)S(1)}, s32[3072]{0:T(1024)}, u32[]{:S(2)}) copy-start(s32[3072]{0:T(1024)} %param.5) | copy-start | bytes 36868
  0.0 6.5 %copy-start.4 = (bf16[3072]{0:T(1024)(128)(2,1)S(1)}, bf16[3072]{0:T(1024)(128)(2,1)}, u32[]{:S(2)}) copy-start(bf16[3072]{0:T(1024)(128)(2,1)} %param.7) | copy-start | bytes 18436
  0.0 20.5 %copy-start.5 = (f32[1024]{0:T(1024)S(1)}, f32[1024]{0:T(1024)}, u32[]{:S(2)}) copy-start(f32[1024]{0:T(1024)} %param.9) | copy-start | bytes 12292
  0.0 20.5 %copy-start.6 = (f32[1024]{0:T(1024)S(1)}, f32[1024]{0:T(1024)}, u32[]{:S(2)}) copy-start(f32[1024]{0:T(1024)} %param.8) | copy-start | bytes 12292
  2.1 31.9 %collective-permute-start.5 = (bf16[1168,128]{1,0:T(8,128)(2,1)S(1)}, bf16[1168,128]{1,0:T(8,128)(2,1)S(1)}, u32[]{:S(2)}, u32[]{:S(2)}) collective-permute-start(bf16[1168,128]{1,0:T(8,128)(2,1)S(1)} %get-tuple-element.11), channel_id=1, source_target_pairs={{0,6},{2,4},{4,2},{6,0},{8,14},{10,12},{12,10},{14,8},{16,22},{18,... | collective-permute-start | bytes 897032 | tf_op jit(solution)/shard_map/ppermute | solution.py:314
  3.6 30.5 %collective-permute-start.4 = (bf16[1168,128]{1,0:T(8,128)(2,1)S(1)}, bf16[1168,128]{1,0:T(8,128)(2,1)S(1)}, u32[]{:S(2)}, u32[]{:S(2)}) collective-permute-start(bf16[1168,128]{1,0:T(8,128)(2,1)S(1)} %get-tuple-element.12), channel_id=1, source_target_pairs={{0,4},{2,6},{4,0},{6,2},{8,12},{10,14},{12,8},{14,10},{16,20},{18,... | collective-permute-start | bytes 897032 | tf_op jit(solution)/shard_map/ppermute | solution.py:314
  5.1 29.0 %collective-permute-start.3 = (bf16[1168,128]{1,0:T(8,128)(2,1)S(1)}, bf16[1168,128]{1,0:T(8,128)(2,1)S(1)}, u32[]{:S(2)}, u32[]{:S(2)}) collective-permute-start(bf16[1168,128]{1,0:T(8,128)(2,1)S(1)} %get-tuple-element.13), channel_id=1, source_target_pairs={{0,2},{2,0},{4,6},{6,4},{8,10},{10,8},{12,14},{14,12},{16,18},{18,... | collective-permute-start | bytes 897032 | tf_op jit(solution)/shard_map/ppermute | solution.py:314
  5.9 15.2 %copy-start.7 = (s32[65]{0:T(128)}, s32[65]{0:T(128)S(1)}, u32[]{:S(2)}) copy-start(s32[65]{0:T(128)S(1)} %convert_reduce_fusion.lows_ref) | copy-start | bytes 784
  11.4 7.6 %collective-permute-start.1 = (f32[17,304]{1,0:T(8,128)S(1)}, f32[17,304]{1,0:T(8,128)S(1)}, u32[]{:S(2)}, u32[]{:S(2)}) collective-permute-start(f32[17,304]{1,0:T(8,128)S(1)} %get-tuple-element.16), channel_id=1, source_target_pairs={{0,4},{2,6},{4,0},{6,2},{8,12},{10,14},{12,8},{14,10},{16,20},{18,... | collective-permute-start | bytes 62024 | tf_op jit(solution)/shard_map/ppermute | solution.py:314
  12.0 20.5 %collective-permute-start = (f32[17,304]{1,0:T(8,128)S(1)}, f32[17,304]{1,0:T(8,128)S(1)}, u32[]{:S(2)}, u32[]{:S(2)}) collective-permute-start(f32[17,304]{1,0:T(8,128)S(1)} %get-tuple-element.16), channel_id=1, source_target_pairs={{0,2},{2,0},{4,6},{6,4},{8,10},{10,8},{12,14},{14,12},{16,18},{18,... | collective-permute-start | bytes 62024 | tf_op jit(solution)/shard_map/ppermute | solution.py:314
  19.0 13.4 %collective-permute-start.2 = (f32[17,304]{1,0:T(8,128)S(1)}, f32[17,304]{1,0:T(8,128)S(1)}, u32[]{:S(2)}, u32[]{:S(2)}) collective-permute-start(f32[17,304]{1,0:T(8,128)S(1)} %get-tuple-element.16), channel_id=1, source_target_pairs={{0,6},{2,4},{4,2},{6,0},{8,14},{10,12},{12,10},{14,8},{16,22},{18,... | collective-permute-start | bytes 62024 | tf_op jit(solution)/shard_map/ppermute | solution.py:314
  34.0 0.7 copy-start
  34.0 0.9 copy-start.1
  34.1 0.9 copy-start.2
